TPU v7x, 128 devices: a whole 4x4x4 slice. The times are simulated.
128 devices in a mesh: dom: 32 (over y, x, core), sub: 4 (over z).
Axes of the slice: x: 4, y: 4, z: 4, core: 2. Of those that a mesh axis runs over, the one named last changes fastest.
Arguments:
- field_state: float32 [9, 20, 32768], P(None, None, ('dom', 'sub')), may hold values from -6 to 6
- adjoint: float32 [9, 20, 32768], P(None, None, ('dom', 'sub')), may hold values from -6 to 6
- eps_inf: float32 [32768], P(('dom', 'sub')), may hold values from 2 to 8
- eps_delta: float32 [32768], P(('dom', 'sub')), may hold values from 2 to 30
- relax_time: float32 [32768], P(('dom', 'sub')), may hold values from 0.2 to 2
- metric: float32 [9, 32768], P(None, ('dom', 'sub')), may hold values from -4 to 4
- face_scale: float32 [4, 32768], P(None, ('dom', 'sub')), may hold values from 0.5 to 2
- face_angles: float32 [2, 4, 32768], P(None, None, ('dom', 'sub')), may hold values from -3.140625 to 3.140625
- nbr_index: int32 [40, 32768], P(None, ('dom', 'sub')), may hold values from 0 to 11263, as said below
- dom_export: int32 [32768], P(('dom', 'sub')), may hold values from 0 to 10239
- sub_export: int32 [128, 4, 128], P(('dom', 'sub')), may hold values from 0 to 10239
- send_slot: int32 [32768], P(('dom', 'sub')), may hold values from 0 to 255, as said below
- recv_index: int32 [128, 128, 2], P(('dom', 'sub')), may hold values from 0 to 64, as said below
Outputs:
- adjoint_out: float32 [9, 20, 32768], P(None, None, ('dom', 'sub'))
- thermal_grad: float32 [3, 8192], P(None, ('dom', 'sub'))
Inputs may be any that keep to these rules, and one draw needn't show every extreme that they name: `nbr_index`: pool rows (10880) to (11135) are never named. `send_slot`: elements of one device that share a slot share a thermal element. `recv_index`: slots that the source leaves empty hold 64.
All inputs are finite; a program needn't handle non-finite values.
Results may differ from a plain program's by a relative error of at most 0.0003.
Values sent between devices are 32-bit elements; how exact they have to be, the bound alone decides.
A program may use at most 128 MiB of HBM per device.

v0:
```python
import math

import jax
import jax.numpy as jnp
from jax import lax
from jax.sharding import PartitionSpec as P

time_step = 0.014


def extended(block, sides, width):
    for axis, dim in sides:
        count = lax.axis_size(axis)
        forward = [(i, i + 1) for i in range(count - 1)]
        backward = [(target, source) for source, target in forward]
        low = lax.ppermute(
            lax.slice_in_dim(block, block.shape[dim] - width, None, axis=dim), axis, forward
        )
        high = lax.ppermute(lax.slice_in_dim(block, 0, width, axis=dim), axis, backward)
        block = jnp.concatenate([low, block, high], axis=dim)
    return block


def mat_mul(left, right):
    inner = len(right)
    return [
        [
            sum((left[row_no][k] * right[k][col_no] for k in range(inner)))
            for col_no in range(len(right[0]))
        ]
        for row_no in range(len(left))
    ]


def transposed(matrix):
    return [list(column) for column in zip(*matrix)]


def solve_linear(matrix, rhs_rows):
    order = len(matrix)
    work = [list(matrix[row_no]) + list(rhs_rows[row_no]) for row_no in range(order)]
    for col_no in range(order):

        def magnitude(row_no):
            return abs(work[row_no][col_no])

        pivot = max(range(col_no, order), key=magnitude)
        work[col_no], work[pivot] = (work[pivot], work[col_no])
        head = work[col_no][col_no]
        work[col_no] = [value / head for value in work[col_no]]
        for row_no in range(order):
            if row_no != col_no:
                factor = work[row_no][col_no]
                work[row_no] = [
                    value - factor * other for value, other in zip(work[row_no], work[col_no])
                ]
    return [row[order:] for row in work]


def reference_element():
    lattice = [(i, j, k) for k in range(4) for j in range(4 - k) for i in range(4 - j - k)]
    points = [[float(v) / 3.0 for v in node] for node in lattice]
    vander = [[0.0] * 20 for node_no in range(20)]
    slopes = [[[0.0] * 20 for node_no in range(20)] for axis_no in range(3)]
    for node_no in range(20):
        for mono_no in range(20):
            power = lattice[mono_no]
            value = 1.0
            for axis_no in range(3):
                value *= points[node_no][axis_no] ** power[axis_no]
            vander[node_no][mono_no] = value
            for axis_no in range(3):
                if power[axis_no] > 0:
                    term = float(power[axis_no])
                    for other_no in range(3):
                        expo_val = power[other_no] - (1 if other_no == axis_no else 0)
                        term *= points[node_no][other_no] ** expo_val
                    slopes[axis_no][node_no][mono_no] = term
    identity = [[1.0 if row_no == col_no else 0.0 for col_no in range(20)] for row_no in range(20)]
    inverse = solve_linear(vander, identity)
    deriv_mats = [mat_mul(slopes[axis_no], inverse) for axis_no in range(3)]
    fact = math.factorial

    def face_integral(face_no, a, b, c):
        if face_no == 0:
            return 0.0 if c > 0 else fact(a) * fact(b) / fact(a + b + 2)
        if face_no == 1:
            return 0.0 if b > 0 else fact(a) * fact(c) / fact(a + c + 2)
        if face_no == 2:
            return math.sqrt(3.0) * fact(a) * fact(b) * fact(c) / fact(a + b + c + 2)
        return 0.0 if a > 0 else fact(b) * fact(c) / fact(b + c + 2)

    inverse_t = transposed(inverse)
    mono_mass = [[0.0] * 20 for node_no in range(20)]
    for first_no in range(20):
        for second_no in range(20):
            a = lattice[first_no][0] + lattice[second_no][0]
            b = lattice[first_no][1] + lattice[second_no][1]
            c = lattice[first_no][2] + lattice[second_no][2]
            mono_mass[first_no][second_no] = fact(a) * fact(b) * fact(c) / fact(a + b + c + 3)
    mass_mat = mat_mul(mat_mul(inverse_t, mono_mass), inverse)
    columns = [[] for node_no in range(20)]
    index_list = []
    for face_no in range(4):
        mono_face = [[0.0] * 20 for node_no in range(20)]
        for first_no in range(20):
            for second_no in range(20):
                a = lattice[first_no][0] + lattice[second_no][0]
                b = lattice[first_no][1] + lattice[second_no][1]
                c = lattice[first_no][2] + lattice[second_no][2]
                mono_face[first_no][second_no] = face_integral(face_no, a, b, c)
        face_mass = mat_mul(mat_mul(inverse_t, mono_face), inverse)
        tests = [k == 0 for i, j, k in lattice]
        if face_no == 1:
            tests = [j == 0 for i, j, k in lattice]
        if face_no == 2:
            tests = [i + j + k == 3 for i, j, k in lattice]
        if face_no == 3:
            tests = [i == 0 for i, j, k in lattice]
        chosen = [node_no for node_no in range(20) if tests[node_no]]
        for row_no in range(20):
            columns[row_no].extend([face_mass[row_no][col_no] for col_no in chosen])
        index_list.extend(chosen)
    lift_mat = solve_linear(mass_mat, columns)
    return (deriv_mats, lift_mat, index_list)


def cross_product(left, right):
    return jnp.stack(
        [
            left[1] * right[2] - left[2] * right[1],
            left[2] * right[0] - left[0] * right[2],
            left[0] * right[1] - left[1] * right[0],
        ]
    )


def curl_of(gradient, offset):
    return jnp.stack(
        [
            gradient[1, offset + 2] - gradient[2, offset + 1],
            gradient[2, offset] - gradient[0, offset + 2],
            gradient[0, offset + 1] - gradient[1, offset],
        ]
    )


def element_rhs(fields, neighbour, eps_inf, eps_delta, relax_time, metric, face_scale, face_angles):
    highest = lax.Precision.HIGHEST
    deriv_table, lift_table, face_index = reference_element()
    deriv_mats = jnp.asarray(deriv_table, dtype=jnp.float32)
    lift_mat = jnp.asarray(lift_table, dtype=jnp.float32)
    face_rows = jnp.asarray(face_index, dtype=jnp.int32)
    elements = fields.shape[-1]
    traces = fields[0:6][:, face_rows, :]
    jump_e = traces[0:3] - neighbour[0:3]
    jump_h = traces[3:6] - neighbour[3:6]
    polar_angle = face_angles[0]
    azimuth = face_angles[1]
    normal = jnp.stack(
        [
            jnp.sin(polar_angle) * jnp.cos(azimuth),
            jnp.sin(polar_angle) * jnp.sin(azimuth),
            jnp.cos(polar_angle),
        ]
    )
    normal = jnp.repeat(normal, 10, axis=1)
    scale_rows = jnp.repeat(face_scale, 10, axis=0)
    normal_e = jnp.sum(normal * jump_e, axis=0)
    normal_h = jnp.sum(normal * jump_h, axis=0)
    flux_e = normal * normal_e - jump_e - cross_product(normal, jump_h)
    flux_h = cross_product(normal, jump_e) + normal * normal_h - jump_h
    face_flux = jnp.concatenate([flux_e, flux_h]) * (0.5 * scale_rows)
    lifted = jnp.einsum("nf,cfk->cnk", lift_mat, face_flux, precision=highest)
    derived = jnp.einsum("dij,cjk->dcik", deriv_mats, fields[0:6], precision=highest)
    gradient = jnp.einsum(
        "dik,dcnk->icnk", metric.reshape(3, 3, elements), derived, precision=highest
    )
    current = (eps_delta * fields[0:3] - fields[6:9]) / relax_time
    rhs_e = (curl_of(gradient, 3) + lifted[0:3] - current) / eps_inf
    rhs_h = lifted[3:6] - curl_of(gradient, 0)
    return jnp.concatenate([rhs_e, rhs_h, current])


def per_device(
    field_state,
    adjoint,
    eps_inf,
    eps_delta,
    relax_time,
    metric,
    face_scale,
    face_angles,
    nbr_index,
    dom_export,
    sub_export,
    send_slot,
    recv_index,
):
    elements = field_state.shape[-1]
    rows = 40 * elements
    rim_rows = dom_export.shape[0] // 2
    sub_count = lax.axis_size("sub")
    sub_slots = sub_export.shape[2]
    flat_index = nbr_index.reshape(-1)
    export_sub = sub_export[0]
    face_rows = jnp.asarray(reference_element()[2], dtype=jnp.int32)

    def own_traces(fields):
        return fields[0:6][:, face_rows, :].reshape(6, rows)

    def exports(fields):
        traces = own_traces(fields)
        return (traces[:, export_sub], traces[:, dom_export])

    def local_part(fields, from_sub, from_dom, e_inf, e_del, tau):
        pool = jnp.concatenate([own_traces(fields), from_sub.reshape(6, -1), from_dom], axis=1)
        neighbour = pool[:, flat_index].reshape(6, 40, elements)
        return element_rhs(fields, neighbour, e_inf, e_del, tau, metric, face_scale, face_angles)

    def swap_rims(values):
        return extended(values, (("dom", 1),), rim_rows)

    def rims_back(cotangent):
        outgoing = jnp.concatenate([cotangent[:, :rim_rows], cotangent[:, 3 * rim_rows :]], axis=1)
        returned = swap_rims(outgoing)
        return jnp.concatenate([returned[:, :rim_rows], returned[:, 3 * rim_rows :]], axis=1)

    def sub_trade(values, backward):
        if backward:
            spread = jnp.zeros((6, sub_count, sub_count, sub_slots), jnp.float32)
            spread = lax.dynamic_update_slice(
                spread, values[:, :, None, :], (0, 0, lax.axis_index("sub"), 0)
            )
            return lax.psum_scatter(
                spread.reshape(6, sub_count * sub_count, sub_slots),
                "sub",
                scatter_dimension=1,
                tiled=True,
            )
        whole = lax.all_gather(values, "sub", axis=1, tiled=True).reshape(
            6, sub_count, sub_count, sub_slots
        )
        return lax.dynamic_index_in_dim(whole, lax.axis_index("sub"), 2, keepdims=False)

    def fetch(fields):
        to_sub, to_dom = exports(fields)
        return (sub_trade(to_sub, False), swap_rims(to_dom))

    sub_one, dom_one = fetch(field_state)
    slope_one = local_part(field_state, sub_one, dom_one, eps_inf, eps_delta, relax_time)
    section_two = field_state + 0.5 * time_step * slope_one
    sub_two, dom_two = fetch(section_two)
    slope_two = local_part(section_two, sub_two, dom_two, eps_inf, eps_delta, relax_time)
    section_three = field_state + 0.5 * time_step * slope_two
    sub_three, dom_three = fetch(section_three)
    slope_three = local_part(section_three, sub_three, dom_three, eps_inf, eps_delta, relax_time)
    section_four = field_state + time_step * slope_three
    sub_four, dom_four = fetch(section_four)
    _, export_pull = jax.vjp(exports, field_state)

    def backward(fields, from_sub, from_dom, weight):
        _, pullback = jax.vjp(
            local_part, fields, from_sub, from_dom, eps_inf, eps_delta, relax_time
        )
        direct, sub_cot, dom_cot, grad_inf, grad_delta, grad_tau = pullback(weight)
        (through,) = export_pull((sub_trade(sub_cot, True), rims_back(dom_cot)))
        return (direct + through, jnp.stack([grad_inf, grad_delta, grad_tau]))

    weight_four = time_step / 6.0 * adjoint
    back_four, grads_four = backward(section_four, sub_four, dom_four, weight_four)
    weight_three = time_step / 3.0 * adjoint + time_step * back_four
    back_three, grads_three = backward(section_three, sub_three, dom_three, weight_three)
    weight_two = time_step / 3.0 * adjoint + 0.5 * time_step * back_three
    back_two, grads_two = backward(section_two, sub_two, dom_two, weight_two)
    weight_one = time_step / 6.0 * adjoint + 0.5 * time_step * back_two
    back_one, grads_one = backward(field_state, sub_one, dom_one, weight_one)
    adjoint_out = adjoint + back_one + back_two + back_three + back_four
    element_grads = grads_one + grads_two + grads_three + grads_four
    dom_count = lax.axis_size("dom")
    devices = dom_count * sub_count
    slots = recv_index.shape[2]
    packed = (
        jnp.zeros((3, devices * slots), jnp.float32)
        .at[:, send_slot]
        .add(element_grads)
        .reshape(3, devices, slots)
    )
    arrived = lax.all_to_all(packed, ("dom", "sub"), split_axis=1, concat_axis=1, tiled=True)
    owned = elements // 4
    thermal_grad = (
        jnp.zeros((3, owned + 1), jnp.float32)
        .at[:, recv_index[0].reshape(-1)]
        .add(arrived.reshape(3, -1))[:, :owned]
    )
    return (adjoint_out, thermal_grad)


def solution(mesh):
    return jax.shard_map(
        per_device,
        mesh=mesh,
        in_specs=(
            P(None, None, ("dom", "sub")),
            P(None, None, ("dom", "sub")),
            P(("dom", "sub")),
            P(("dom", "sub")),
            P(("dom", "sub")),
            P(None, ("dom", "sub")),
            P(None, ("dom", "sub")),
            P(None, None, ("dom", "sub")),
            P(None, ("dom", "sub")),
            P(("dom", "sub")),
            P(("dom", "sub"), None, None),
            P(("dom", "sub")),
            P(("dom", "sub"), None, None),
        ),
        out_specs=(P(None, None, ("dom", "sub")), P(None, ("dom", "sub"))),
        check_vma=False,
    )
```

profile of v0, /device:TPU:1, one launch (start us, length us, event | category | flops | bytes accessed | tf_op | source)
XLA Modules:
  0.0 1025.2 jit_solution(3849606152104193809)
XLA Ops:
  17.2 4.5 collective-permute-start.8
  23.7 4.4 constant_dynamic-update-slice_fusion.4
  33.1 10.2 all-gather
  50.6 8.9 convolution_bitcast_fusion.3
  59.5 7.0 fusion.183
  79.4 37.1 %gather_fusion.3 = f32[10240,6]{1,0:T(8,128)} fusion(f32[6,11264]{0,1:T(8,128)} %constant_dynamic-update-slice_fusion, s32[10240]{0:T(1024)S(1)} %broadcast_clamp_fusion), kind=kCustom, calls=%fused_computation.3 | custom fusion | bytes 532480 | tf_op jit(solution)/shard_map/jvp()/gather | solution.py:218
  116.5 8.8 fusion.176
  137.6 57.9 %scatter_custom_fusion.1 = f32[6,11264]{0,1:T(8,128)} fusion(s32[10240]{0:T(1024)} %bitcast.525, f32[10240,6]{1,0:T(8,128)} %bitcast.482, f32[]{:T(128)} %constant.20.clone.1), kind=kCustom, calls=%fused_computation.48 | custom fusion | flops 61440 | bytes 270848 | tf_op jit(solution)/shard_map/transpose(jvp())/scatter-add | solution.py:218
  198.0 6.5 collective-permute-start
  206.7 4.6 split.121
  225.8 13.4 %reduce-scatter.5.cloned.1.call-done = f32[6,4,128]{0,2,1:T(8,128)} async-done(((f32[6,16,128]{0,2,1:T(8,128)}), f32[6,4,128]{0,2,1:T(8,128)}) %reduce-scatter.5.cloned.1.call-update) | async-done | bytes 12304 | tf_op jit(solution)/shard_map/reduce_scatter | solution.py:235
  239.3 5.3 scatter_custom_fusion.4
  244.6 6.5 add_any.441
  279.8 9.3 all-gather.1
  289.9 7.6 collective-permute-start.10
  303.5 7.5 convolution_bitcast_fusion.2
  316.9 8.4 fusion.184
  332.6 37.1 %gather_fusion.7 = f32[10240,6]{1,0:T(8,128)} fusion(f32[6,11264]{0,1:T(8,128)} %constant_dynamic-update-slice_fusion.5, s32[10240]{0:T(1024)S(1)} %broadcast_clamp_fusion), kind=kCustom, calls=%fused_computation.7 | custom fusion | bytes 532480 | tf_op jit(solution)/shard_map/jvp()/gather | solution.py:218
  369.7 8.8 fusion.175
  389.3 58.1 %scatter_custom_fusion.7 = f32[6,11264]{0,1:T(8,128)} fusion(s32[10240]{0:T(1024)} %bitcast.526, f32[10240,6]{1,0:T(8,128)} %bitcast.483, f32[]{:T(128)} %constant.20.clone.1), kind=kCustom, calls=%fused_computation.46 | custom fusion | flops 61440 | bytes 270848 | tf_op jit(solution)/shard_map/transpose(jvp())/scatter-add | solution.py:218
  458.0 4.3 split.128
  476.8 11.8 %reduce-scatter.7.cloned.1.call-done = f32[6,4,128]{0,2,1:T(8,128)} async-done(((f32[6,16,128]{0,2,1:T(8,128)}), f32[6,4,128]{0,2,1:T(8,128)}) %reduce-scatter.7.cloned.1.call-update) | async-done | bytes 12304 | tf_op jit(solution)/shard_map/reduce_scatter | solution.py:235
  488.6 5.3 scatter_custom_fusion.10
  493.9 6.9 add_any.475
  531.7 7.6 convolution_bitcast_fusion.1
  542.4 9.3 all-gather.2
  553.3 7.5 collective-permute-start.12
  565.0 8.4 fusion.185
  584.2 37.1 %gather_fusion.11 = f32[10240,6]{1,0:T(8,128)} fusion(f32[6,11264]{0,1:T(8,128)} %constant_dynamic-update-slice_fusion.10, s32[10240]{0:T(1024)S(1)} %broadcast_clamp_fusion), kind=kCustom, calls=%fused_computation.11 | custom fusion | bytes 532480 | tf_op jit(solution)/shard_map/jvp()/gather | solution.py:218
  621.4 8.8 fusion.174
  642.1 57.9 %scatter_custom_fusion.13 = f32[6,11264]{0,1:T(8,128)} fusion(s32[10240]{0:T(1024)} %bitcast.527, f32[10240,6]{1,0:T(8,128)} %bitcast.484, f32[]{:T(128)} %constant.20.clone.1), kind=kCustom, calls=%fused_computation.44 | custom fusion | flops 61440 | bytes 270848 | tf_op jit(solution)/shard_map/transpose(jvp())/scatter-add | solution.py:218
  709.0 4.5 split.135
  728.9 13.7 %reduce-scatter.9.cloned.1.call-done = f32[6,4,128]{0,2,1:T(8,128)} async-done(((f32[6,16,128]{0,2,1:T(8,128)}), f32[6,4,128]{0,2,1:T(8,128)}) %reduce-scatter.9.cloned.1.call-update) | async-done | bytes 12304 | tf_op jit(solution)/shard_map/reduce_scatter | solution.py:235
  742.6 5.3 scatter_custom_fusion.16
  747.9 6.5 add_any.509
  784.5 9.3 all-gather.3
  794.6 7.6 collective-permute-start.14
  805.5 8.3 fusion.186
  819.9 7.5 convolution_bitcast_fusion
  836.8 37.3 %gather_fusion.15 = f32[10240,6]{1,0:T(8,128)} fusion(f32[6,11264]{0,1:T(8,128)} %constant_dynamic-update-slice_fusion.15, s32[10240]{0:T(1024)S(1)} %broadcast_clamp_fusion), kind=kCustom, calls=%fused_computation.15 | custom fusion | bytes 532480 | tf_op jit(solution)/shard_map/jvp()/gather | solution.py:218
  874.1 8.8 fusion.173
  893.1 57.9 %scatter_custom_fusion.19 = f32[6,11264]{0,1:T(8,128)} fusion(s32[10240]{0:T(1024)} %bitcast.528, f32[10240,6]{1,0:T(8,128)} %bitcast.481, f32[]{:T(128)} %constant.20.clone.1), kind=kCustom, calls=%fused_computation.42 | custom fusion | flops 61440 | bytes 270848 | tf_op jit(solution)/shard_map/transpose(jvp())/scatter-add | solution.py:218
  955.0 8.8 all-to-all-start
  969.5 4.7 split.142
  985.0 4.4 scatter_custom_fusion.21
  989.4 10.7 %reduce-scatter.11.cloned.1.call-done = f32[6,4,128]{0,2,1:T(8,128)} async-done(((f32[6,16,128]{0,2,1:T(8,128)}), f32[6,4,128]{0,2,1:T(8,128)}) %reduce-scatter.11.cloned.1.call-update) | async-done | bytes 12304 | tf_op jit(solution)/shard_map/reduce_scatter | solution.py:235
  1000.1 5.3 scatter_custom_fusion.22
  1005.4 6.5 add_any.543
  (574 shorter events, 324.9 us)
Async XLA Ops:
  7.2 232.1 %reduce-scatter.5.cloned.1.call-start = ((), (), s32[]{:S(2)}) async-start(), calls=%async_computation.5 | async-start | bytes 1310720 | tf_op jit(solution)/shard_map/reduce_scatter | solution.py:235
  7.9 20.2 %copy-start.104 = (s32[512]{0:T(512)}, s32[512]{0:T(512)S(1)}, u32[]{:S(2)}) copy-start(s32[512]{0:T(512)S(1)} %fusion.121) | copy-start | bytes 6148
  9.6 19.9 %copy-start.91 = (s32[1024]{0:T(1024)}, s32[1024]{0:T(1024)S(1)}, u32[]{:S(2)}) copy-start(s32[1024]{0:T(1024)S(1)} %get-tuple-element.386) | copy-start | bytes 12292
  17.2 60.2 %collective-permute-start.8 = (f32[6,128]{0,1:T(8,128)S(1)}, f32[6,128]{0,1:T(8,128)S(1)}, u32[]{:S(2)}, u32[]{:S(2)}) collective-permute-start(f32[6,128]{0,1:T(8,128)S(1)} %get-tuple-element.263), channel_id=1, source_target_pairs={{0,4},{4,8},{8,12},{12,16},{16,20},{20,24},{24,28},{28,32},{32,36}... | collective-permute-start | bytes 9224 | tf_op jit(solution)/shard_map/ppermute | solution.py:16
  21.7 57.0 %collective-permute-start.9 = (f32[6,128]{0,1:T(8,128)S(1)}, f32[6,128]{0,1:T(8,128)S(1)}, u32[]{:S(2)}, u32[]{:S(2)}) collective-permute-start(f32[6,128]{0,1:T(8,128)S(1)} %get-tuple-element.262), channel_id=1, source_target_pairs={{4,0},{8,4},{12,8},{16,12},{20,16},{24,20},{28,24},{32,28},{36,32}... | collective-permute-start | bytes 9224 | tf_op jit(solution)/shard_map/ppermute | solution.py:19
  23.7 19.8 %copy-start.90 = (s32[40,256]{1,0:T(8,128)S(1)}, s32[40,256]{1,0:T(8,128)}, u32[]{:S(2)}) copy-start(s32[40,256]{1,0:T(8,128)} %param.43) | copy-start | bytes 122884
  23.7 19.9 %copy-start.112 = (f32[4,256]{1,0:T(4,128)S(1)}, f32[4,256]{1,0:T(4,128)}, u32[]{:S(2)}) copy-start(f32[4,256]{1,0:T(4,128)} %param.41) | copy-start | bytes 12292
  23.7 20.0 %copy-start.103 = (f32[2,4,256]{2,1,0:T(4,128)S(1)}, f32[2,4,256]{2,1,0:T(4,128)}, u32[]{:S(2)}) copy-start(f32[2,4,256]{2,1,0:T(4,128)} %param.42) | copy-start | bytes 24580
  28.1 19.1 %copy-start.1 = (f32[9,20,256]{2,1,0:T(8,128)S(1)}, f32[9,20,256]{2,1,0:T(8,128)}, u32[]{:S(2)}) copy-start(f32[9,20,256]{2,1,0:T(8,128)} %param.35) | copy-start | bytes 552964
  28.1 19.0 %copy-start.95 = (f32[3,20,20,1]{1,2,3,0:T(8,128)S(1)}, f32[3,20,20,1]{1,2,3,0:T(8,128)}, u32[]{:S(2)}) copy-start(f32[3,20,20,1]{1,2,3,0:T(8,128)} %constant.374) | copy-start | bytes 14404
  28.2 22.4 %copy-start.10 = (f32[9,20,256]{2,1,0:T(8,128)}, f32[9,20,256]{2,1,0:T(8,128)S(1)}, u32[]{:S(2)}) copy-start(f32[9,20,256]{2,1,0:T(8,128)S(1)} %broadcast_multiply_fusion) | copy-start | bytes 552964
  28.8 47.2 %copy-start.21 = (f32[3,20,256]{2,1,0:T(8,128)}, f32[3,20,256]{2,1,0:T(8,128)S(1)}, u32[]{:S(2)}) copy-start(f32[3,20,256]{2,1,0:T(8,128)S(1)} %get-tuple-element.202) | copy-start | bytes 184324
  28.8 47.9 %copy-start.7 = (f32[3,20,256]{2,1,0:T(8,128)}, f32[3,20,256]{2,1,0:T(8,128)S(1)}, u32[]{:S(2)}) copy-start(f32[3,20,256]{2,1,0:T(8,128)S(1)} %get-tuple-element.203) | copy-start | bytes 184324
  137.6 69.0 %copy-start.32 = (f32[3,40,256]{2,1,0:T(8,128)S(1)}, f32[3,40,256]{2,1,0:T(8,128)}, u32[]{:S(2)}) copy-start(f32[3,40,256]{2,1,0:T(8,128)} %get-tuple-element.134) | copy-start | bytes 368644
  198.0 21.6 %collective-permute-start = (f32[6,128]{0,1:T(8,128)}, f32[6,128]{0,1:T(8,128)}, u32[]{:S(2)}, u32[]{:S(2)}) collective-permute-start(f32[6,128]{0,1:T(8,128)} %get-tuple-element.96), channel_id=1, source_target_pairs={{0,4},{4,8},{8,12},{12,16},{16,20},{20,24},{24,28},{28,32},{32,36}... | collective-permute-start | bytes 9224 | tf_op jit(solution)/shard_map/ppermute | solution.py:16
  204.6 16.0 %collective-permute-start.1 = (f32[6,128]{0,1:T(8,128)}, f32[6,128]{0,1:T(8,128)}, u32[]{:S(2)}, u32[]{:S(2)}) collective-permute-start(f32[6,128]{0,1:T(8,128)} %get-tuple-element.97), channel_id=1, source_target_pairs={{4,0},{8,4},{12,8},{16,12},{20,16},{24,20},{28,24},{32,28},{36,32}... | collective-permute-start | bytes 9224 | tf_op jit(solution)/shard_map/ppermute | solution.py:19
  213.9 274.8 %reduce-scatter.7.cloned.1.call-start = ((), (), s32[]{:S(2)}) async-start(), calls=%async_computation.6 | async-start | bytes 1310720 | tf_op jit(solution)/shard_map/reduce_scatter | solution.py:235
  275.9 23.6 %copy-start.28 = (f32[256,6]{1,0:T(8,128)}, f32[256,6]{1,0:T(8,128)S(1)}, u32[]{:S(2)}) copy-start(f32[256,6]{1,0:T(8,128)S(1)} %gather_fusion.6) | copy-start | bytes 18436
  289.9 39.9 %collective-permute-start.10 = (f32[6,128]{0,1:T(8,128)}, f32[6,128]{0,1:T(8,128)}, u32[]{:S(2)}, u32[]{:S(2)}) collective-permute-start(f32[6,128]{0,1:T(8,128)} %get-tuple-element.261), channel_id=1, source_target_pairs={{0,4},{4,8},{8,12},{12,16},{16,20},{20,24},{24,28},{28,32},{32,36}... | collective-permute-start | bytes 9224 | tf_op jit(solution)/shard_map/ppermute | solution.py:16
  297.6 34.4 %collective-permute-start.11 = (f32[6,128]{0,1:T(8,128)}, f32[6,128]{0,1:T(8,128)S(1)}, u32[]{:S(2)}, u32[]{:S(2)}) collective-permute-start(f32[6,128]{0,1:T(8,128)} %get-tuple-element.260), channel_id=1, source_target_pairs={{4,0},{8,4},{12,8},{16,12},{20,16},{24,20},{28,24},{32,28},{36,32}... | collective-permute-start | bytes 9224 | tf_op jit(solution)/shard_map/ppermute | solution.py:19
  450.0 20.7 %collective-permute-start.2 = (f32[6,128]{0,1:T(8,128)}, f32[6,128]{0,1:T(8,128)}, u32[]{:S(2)}, u32[]{:S(2)}) collective-permute-start(f32[6,128]{0,1:T(8,128)} %get-tuple-element.94), channel_id=1, source_target_pairs={{0,4},{4,8},{8,12},{12,16},{16,20},{20,24},{24,28},{28,32},{32,36}... | collective-permute-start | bytes 9224 | tf_op jit(solution)/shard_map/ppermute | solution.py:16
  453.6 17.9 %collective-permute-start.3 = (f32[6,128]{0,1:T(8,128)}, f32[6,128]{0,1:T(8,128)}, u32[]{:S(2)}, u32[]{:S(2)}) collective-permute-start(f32[6,128]{0,1:T(8,128)} %get-tuple-element.95), channel_id=1, source_target_pairs={{4,0},{8,4},{12,8},{16,12},{20,16},{24,20},{28,24},{32,28},{36,32}... | collective-permute-start | bytes 9224 | tf_op jit(solution)/shard_map/ppermute | solution.py:19
  464.8 277.8 %reduce-scatter.9.cloned.1.call-start = ((), (), s32[]{:S(2)}) async-start(), calls=%async_computation.7 | async-start | bytes 1310720 | tf_op jit(solution)/shard_map/reduce_scatter | solution.py:235
  527.4 25.3 %copy-start.30 = (f32[256,6]{1,0:T(8,128)}, f32[256,6]{1,0:T(8,128)S(1)}, u32[]{:S(2)}) copy-start(f32[256,6]{1,0:T(8,128)S(1)} %gather_fusion.10) | copy-start | bytes 18436
  531.7 29.1 %copy-start.39 = (f32[3,20,256]{2,1,0:T(8,128)S(1)}, f32[3,20,256]{2,1,0:T(8,128)}, u32[]{:S(2)}) copy-start(f32[3,20,256]{2,1,0:T(8,128)} %get-tuple-element.187) | copy-start | bytes 184324
  531.7 29.5 %copy-start.38 = (f32[3,20,256]{2,1,0:T(8,128)S(1)}, f32[3,20,256]{2,1,0:T(8,128)}, u32[]{:S(2)}) copy-start(f32[3,20,256]{2,1,0:T(8,128)} %get-tuple-element.189) | copy-start | bytes 184324
  553.3 27.8 %collective-permute-start.12 = (f32[6,128]{0,1:T(8,128)}, f32[6,128]{0,1:T(8,128)}, u32[]{:S(2)}, u32[]{:S(2)}) collective-permute-start(f32[6,128]{0,1:T(8,128)} %get-tuple-element.259), channel_id=1, source_target_pairs={{0,4},{4,8},{8,12},{12,16},{16,20},{20,24},{24,28},{28,32},{32,36}... | collective-permute-start | bytes 9224 | tf_op jit(solution)/shard_map/ppermute | solution.py:16
  578.0 5.6 collective-permute-start.13
  702.5 21.8 %collective-permute-start.4 = (f32[6,128]{0,1:T(8,128)}, f32[6,128]{0,1:T(8,128)S(1)}, u32[]{:S(2)}, u32[]{:S(2)}) collective-permute-start(f32[6,128]{0,1:T(8,128)} %get-tuple-element.92), channel_id=1, source_target_pairs={{0,4},{4,8},{8,12},{12,16},{16,20},{20,24},{24,28},{28,32},{32,36}... | collective-permute-start | bytes 9224 | tf_op jit(solution)/shard_map/ppermute | solution.py:16
  705.8 18.6 %collective-permute-start.5 = (f32[6,128]{0,1:T(8,128)}, f32[6,128]{0,1:T(8,128)S(1)}, u32[]{:S(2)}, u32[]{:S(2)}) collective-permute-start(f32[6,128]{0,1:T(8,128)} %get-tuple-element.93), channel_id=1, source_target_pairs={{4,0},{8,4},{12,8},{16,12},{20,16},{24,20},{28,24},{32,28},{36,32}... | collective-permute-start | bytes 9224 | tf_op jit(solution)/shard_map/ppermute | solution.py:19
  794.6 38.1 %collective-permute-start.14 = (f32[6,128]{0,1:T(8,128)}, f32[6,128]{0,1:T(8,128)}, u32[]{:S(2)}, u32[]{:S(2)}) collective-permute-start(f32[6,128]{0,1:T(8,128)} %get-tuple-element.257), channel_id=1, source_target_pairs={{0,4},{4,8},{8,12},{12,16},{16,20},{20,24},{24,28},{28,32},{32,36}... | collective-permute-start | bytes 9224 | tf_op jit(solution)/shard_map/ppermute | solution.py:16
  830.6 5.6 collective-permute-start.15
  893.0 59.4 %copy-start.8 = (f32[3,20,256]{2,1,0:T(8,128)S(1)}, f32[3,20,256]{2,1,0:T(8,128)}, u32[]{:S(2)}) copy-start(f32[3,20,256]{2,1,0:T(8,128)} %copy-done.7) | copy-start | bytes 184324
  893.0 59.4 %copy-start.11 = (f32[9,20,256]{2,1,0:T(8,128)S(1)}, f32[9,20,256]{2,1,0:T(8,128)}, u32[]{:S(2)}) copy-start(f32[9,20,256]{2,1,0:T(8,128)} %copy-done.10) | copy-start | bytes 552964
  893.0 59.4 %copy-start.22 = (f32[3,20,256]{2,1,0:T(8,128)S(1)}, f32[3,20,256]{2,1,0:T(8,128)}, u32[]{:S(2)}) copy-start(f32[3,20,256]{2,1,0:T(8,128)} %copy-done.21) | copy-start | bytes 184324
  893.0 59.4 %copy-start.35 = (f32[3,20,256]{2,1,0:T(8,128)S(1)}, f32[3,20,256]{2,1,0:T(8,128)}, u32[]{:S(2)}) copy-start(f32[3,20,256]{2,1,0:T(8,128)} %get-tuple-element.182) | copy-start | bytes 184324
  893.0 59.4 %copy-start.84 = (f32[256]{0:T(256)S(1)}, f32[256]{0:T(256)}, u32[]{:S(2)}) copy-start(f32[256]{0:T(256)} %param.39) | copy-start | bytes 3076
  893.1 59.4 %copy-start.89 = (f32[256]{0:T(256)S(1)}, f32[256]{0:T(256)}, u32[]{:S(2)}) copy-start(f32[256]{0:T(256)} %param.38) | copy-start | bytes 3076
  893.1 59.4 %copy-start.97 = (f32[256]{0:T(256)S(1)}, f32[256]{0:T(256)}, u32[]{:S(2)}) copy-start(f32[256]{0:T(256)} %get-tuple-element.388) | copy-start | bytes 3076
  893.1 59.4 %copy-start.99 = (f32[256]{0:T(256)S(1)}, f32[256]{0:T(256)}, u32[]{:S(2)}) copy-start(f32[256]{0:T(256)} %get-tuple-element.389) | copy-start | bytes 3076
  893.1 59.5 %copy-start.105 = (f32[256]{0:T(256)S(1)}, f32[256]{0:T(256)}, u32[]{:S(2)}) copy-start(f32[256]{0:T(256)} %get-tuple-element.181) | copy-start | bytes 3076
  893.1 59.5 %copy-start.110 = (f32[256]{0:T(256)S(1)}, f32[256]{0:T(256)}, u32[]{:S(2)}) copy-start(f32[256]{0:T(256)} %neg.624) | copy-start | bytes 3076
  893.1 59.5 %copy-start.111 = (f32[256]{0:T(256)S(1)}, f32[256]{0:T(256)}, u32[]{:S(2)}) copy-start(f32[256]{0:T(256)} %neg.626) | copy-start | bytes 3076
  893.1 59.5 %copy-start.114 = (f32[256]{0:T(256)S(1)}, f32[256]{0:T(256)}, u32[]{:S(2)}) copy-start(f32[256]{0:T(256)} %get-tuple-element.188) | copy-start | bytes 3076
  955.0 27.4 %all-to-all-start = ((f32[3,128,2]{0,2,1:T(2,128)}), f32[3,128,2]{0,2,1:T(2,128)S(1)}, u32[]{:S(2)}, u32[]{:S(2)}) async-start(f32[3,128,2]{0,2,1:T(2,128)} %bitcast.214), calls=%async_computation.4 | async-start | bytes 262144 | tf_op jit(solution)/shard_map/all_to_all | solution.py:289
  963.8 36.3 %reduce-scatter.11.cloned.1.call-start = ((), (), s32[]{:S(2)}) async-start(), calls=%async_computation.8 | async-start | bytes 1310720 | tf_op jit(solution)/shard_map/reduce_scatter | solution.py:235
  963.8 20.8 %collective-permute-start.6 = (f32[6,128]{0,1:T(8,128)S(1)}, f32[6,128]{0,1:T(8,128)S(1)}, u32[]{:S(2)}, u32[]{:S(2)}) collective-permute-start(f32[6,128]{0,1:T(8,128)S(1)} %get-tuple-element.90), channel_id=1, source_target_pairs={{0,4},{4,8},{8,12},{12,16},{16,20},{20,24},{24,28},{28,32},{32,36}... | collective-permute-start | bytes 9224 | tf_op jit(solution)/shard_map/ppermute | solution.py:16
  967.4 17.4 %collective-permute-start.7 = (f32[6,128]{0,1:T(8,128)S(1)}, f32[6,128]{0,1:T(8,128)S(1)}, u32[]{:S(2)}, u32[]{:S(2)}) collective-permute-start(f32[6,128]{0,1:T(8,128)S(1)} %get-tuple-element.91), channel_id=1, source_target_pairs={{4,0},{8,4},{12,8},{16,12},{20,16},{24,20},{28,24},{32,28},{36,32}... | collective-permute-start | bytes 9224 | tf_op jit(solution)/shard_map/ppermute | solution.py:19
  (94 other events, 820.4 us)
Sparse Core Ops, SparseCore 0:
  214.0 25.2 reduce-scatter.4
  464.9 23.6 reduce-scatter.6
  718.7 23.7 reduce-scatter.8
  976.8 23.2 reduce-scatter.10
where the time goes:
time: 1030 us
  local copies, waits for them, and re-layouts  404 us (39%)
  other arithmetic  365 us (35%)
  matrix products  81.7 us (8%)
  starting transfers between devices  68.6 us (7%)
  waiting for transfers between devices  51.5 us (5%)
  blocking collectives  38 us (4%)
  between operations  16.6 us (2%)
    scatter-add x4, other arithmetic, local_part(): neighbour = pool[:, flat_index].reshape(6, 40, elements)  232 us
    gather x4, local copies, waits for them, and re-layouts, local_part(): neighbour = pool[:, flat_index].reshape(6, 40, elements)  149 us
    dot_general x8, matrix products, element_rhs(): jnp.einsum('dik,dcnk->icnk', metric.reshape(3, 3, elements), derived, pre...  63.6 us
    reduce_scatter x4, waiting for transfers between devices, sub_trade(): lax.psum_scatter(spread.reshape(6, sub_count * sub_count, sub_slots), 'su...  49.7 us
    slice x8, local copies, waits for them, and re-layouts, element_rhs(): jump_e = traces[0:3] - neighbour[0:3]  48.4 us
    ppermute x8, starting transfers between devices, extended(): lax.ppermute(lax.slice_in_dim(block, block.shape[dim] - width, None, axis...  44.3 us
    reshape x12, local copies, waits for them, and re-layouts, own_traces(): return fields[0:6][:, face_rows, :].reshape(6, rows)  39.7 us
    scatter-add x8, other arithmetic, exports(): return (traces[:, export_sub], traces[:, dom_export])  38.2 us
  transfers between devices with their start and end apart: 21, of which 6 were waited for; matrix products, arithmetic and copies ran while one was open for 20% of the time, Pallas kernels for 0%

commit v1 on v0

v1 whole, which is shorter than its diff:
```python
import math

import jax
import jax.numpy as jnp
import numpy as np
from jax import lax
from jax.experimental import pallas as pl
from jax.experimental.pallas import tpu as pltpu
from jax.sharding import PartitionSpec as P

time_step = 0.014
f32 = jnp.float32
bf16 = jnp.bfloat16
NODES = 20
ROWS = 24
FACE = 40
DOMS = 32
SUBS = 4
BLOCKS = 6
MESH = pl.DeviceIdType.MESH


def mat_mul(left, right):
    inner = len(right)
    return [
        [
            sum((left[row_no][k] * right[k][col_no] for k in range(inner)))
            for col_no in range(len(right[0]))
        ]
        for row_no in range(len(left))
    ]


def transposed(matrix):
    return [list(column) for column in zip(*matrix)]


def solve_linear(matrix, rhs_rows):
    order = len(matrix)
    work = [list(matrix[row_no]) + list(rhs_rows[row_no]) for row_no in range(order)]
    for col_no in range(order):

        def magnitude(row_no):
            return abs(work[row_no][col_no])

        pivot = max(range(col_no, order), key=magnitude)
        work[col_no], work[pivot] = (work[pivot], work[col_no])
        head = work[col_no][col_no]
        work[col_no] = [value / head for value in work[col_no]]
        for row_no in range(order):
            if row_no != col_no:
                factor = work[row_no][col_no]
                work[row_no] = [
                    value - factor * other for value, other in zip(work[row_no], work[col_no])
                ]
    return [row[order:] for row in work]


def reference_element():
    lattice = [(i, j, k) for k in range(4) for j in range(4 - k) for i in range(4 - j - k)]
    points = [[float(v) / 3.0 for v in node] for node in lattice]
    vander = [[0.0] * 20 for node_no in range(20)]
    slopes = [[[0.0] * 20 for node_no in range(20)] for axis_no in range(3)]
    for node_no in range(20):
        for mono_no in range(20):
            power = lattice[mono_no]
            value = 1.0
            for axis_no in range(3):
                value *= points[node_no][axis_no] ** power[axis_no]
            vander[node_no][mono_no] = value
            for axis_no in range(3):
                if power[axis_no] > 0:
                    term = float(power[axis_no])
                    for other_no in range(3):
                        expo_val = power[other_no] - (1 if other_no == axis_no else 0)
                        term *= points[node_no][other_no] ** expo_val
                    slopes[axis_no][node_no][mono_no] = term
    identity = [[1.0 if row_no == col_no else 0.0 for col_no in range(20)] for row_no in range(20)]
    inverse = solve_linear(vander, identity)
    deriv_mats = [mat_mul(slopes[axis_no], inverse) for axis_no in range(3)]
    fact = math.factorial

    def face_integral(face_no, a, b, c):
        if face_no == 0:
            return 0.0 if c > 0 else fact(a) * fact(b) / fact(a + b + 2)
        if face_no == 1:
            return 0.0 if b > 0 else fact(a) * fact(c) / fact(a + c + 2)
        if face_no == 2:
            return math.sqrt(3.0) * fact(a) * fact(b) * fact(c) / fact(a + b + c + 2)
        return 0.0 if a > 0 else fact(b) * fact(c) / fact(b + c + 2)

    inverse_t = transposed(inverse)
    mono_mass = [[0.0] * 20 for node_no in range(20)]
    for first_no in range(20):
        for second_no in range(20):
            a = lattice[first_no][0] + lattice[second_no][0]
            b = lattice[first_no][1] + lattice[second_no][1]
            c = lattice[first_no][2] + lattice[second_no][2]
            mono_mass[first_no][second_no] = fact(a) * fact(b) * fact(c) / fact(a + b + c + 3)
    mass_mat = mat_mul(mat_mul(inverse_t, mono_mass), inverse)
    columns = [[] for node_no in range(20)]
    index_list = []
    for face_no in range(4):
        mono_face = [[0.0] * 20 for node_no in range(20)]
        for first_no in range(20):
            for second_no in range(20):
                a = lattice[first_no][0] + lattice[second_no][0]
                b = lattice[first_no][1] + lattice[second_no][1]
                c = lattice[first_no][2] + lattice[second_no][2]
                mono_face[first_no][second_no] = face_integral(face_no, a, b, c)
        face_mass = mat_mul(mat_mul(inverse_t, mono_face), inverse)
        tests = [k == 0 for i, j, k in lattice]
        if face_no == 1:
            tests = [j == 0 for i, j, k in lattice]
        if face_no == 2:
            tests = [i + j + k == 3 for i, j, k in lattice]
        if face_no == 3:
            tests = [i == 0 for i, j, k in lattice]
        chosen = [node_no for node_no in range(20) if tests[node_no]]
        for row_no in range(20):
            columns[row_no].extend([face_mass[row_no][col_no] for col_no in chosen])
        index_list.extend(chosen)
    lift_mat = solve_linear(mass_mat, columns)
    return (deriv_mats, lift_mat, index_list)


def host_tables():
    deriv, lift, faces = reference_element()
    deriv = np.asarray(deriv, np.float32)
    lift = np.asarray(lift, np.float32)
    pick = np.zeros((NODES, FACE), np.float32)
    pick[np.asarray(faces), np.arange(FACE)] = 1.0

    def placed(rows, cols, parts):
        result = np.zeros((rows, cols), np.float32)
        for at, part in parts:
            result[: part.shape[0], at : at + part.shape[1]] = part
        return result

    forward = placed(ROWS, 112, [(0, lift)] + [(40 + 24 * d, deriv[d]) for d in range(3)])
    backward = placed(ROWS, 112, [(0, pick)] + [(40 + 24 * d, deriv[d].T) for d in range(3)])
    lift_t = placed(FACE, ROWS, [(0, lift.T)])
    pick_t = placed(FACE, ROWS, [(0, pick.T)])

    def split(matrix):
        high = matrix.astype(jnp.bfloat16).astype(np.float32)
        low = matrix - high
        return np.concatenate(
            [np.concatenate([high, high], 1), np.concatenate([low, np.zeros_like(low)], 1)], 0
        )

    table = np.zeros((224, 256), np.float32)
    table[0:48, 0:224] = split(forward)
    table[48:96, 0:224] = split(backward)
    table[96:176, 0:48] = split(lift_t)
    table[176:216, 0:48] = np.concatenate([pick_t, pick_t], 1)
    return table.astype(jnp.bfloat16), [int(v) for v in faces]


def stacked(values):
    high = values.astype(bf16).astype(f32)
    return jnp.concatenate([high, values - high], axis=0).astype(bf16)


def parts3(values):
    first = values.astype(bf16)
    rest = values - first.astype(f32)
    second = rest.astype(bf16)
    third = (rest - second.astype(f32)).astype(bf16)
    return first, second, third


def dot(left, right):
    return jnp.dot(left, right, preferred_element_type=f32)


def node_of(rows, faces):
    result = rows - 20
    for row, node in enumerate(faces):
        result = jnp.where(rows == row, node, result)
    return result


def one_hot(condition):
    return jnp.where(condition, 1.0, 0.0).astype(bf16)


def kernel_of(faces):
    def kernel(
        fs, adj, einf, edel, tau, met, fsc, ang, nbr, dexp, sexp, sslot, recv, tab,
        out, therm,
        y, k, w, adj24, acc, nrm, scl, x, p, nb, cd, s_ref, pool, pp, nodes, nodex,
        a_mat, at_mat, ax, axt, b_mat, bx,
        sf, rf, sb, rb, ya, yr, cb, rc,
        fs_sem, fr_sem, bs_sem, br_sem, ps_sem, pr_sem, qs_sem, qr_sem,
    ):
        dom = lax.axis_index("dom")
        sub = lax.axis_index("sub")

        rf[...] = jnp.zeros_like(rf)
        rb[...] = jnp.zeros_like(rb)
        yr[...] = jnp.zeros_like(yr)
        rc[...] = jnp.zeros_like(rc)
        barrier = pltpu.get_barrier_semaphore()
        for step in range(1, SUBS):
            pl.semaphore_signal(
                barrier, inc=1, device_id=(dom, lax.rem(sub + step, SUBS)), device_id_type=MESH
            )

        def greet(step, carry):
            pl.semaphore_signal(
                barrier, inc=1, device_id=(lax.rem(dom + step, DOMS), sub), device_id_type=MESH
            )
            return carry

        lax.fori_loop(1, DOMS, greet, 0)

        ie = 1.0 / einf[...]
        it = 1.0 / tau[...]
        ed = edel[...]
        pad = jnp.zeros((ROWS - NODES, 256), f32)
        for c in range(9):
            y[0, c] = jnp.concatenate([fs[c], pad], axis=0)
            value = jnp.concatenate([adj[c], pad], axis=0)
            adj24[c] = value
            acc[c] = value
            w[0, c] = (time_step / 6.0) * value
        sin_a = jnp.sin(ang[0])
        normals = (sin_a * jnp.cos(ang[1]), sin_a * jnp.sin(ang[1]), jnp.cos(ang[0]))
        for face in range(4):
            here = slice(10 * face, 10 * face + 10)
            for i in range(3):
                nrm[i, here, :] = jnp.broadcast_to(normals[i][face : face + 1], (10, 256))
            scl[here, :] = jnp.broadcast_to(0.5 * fsc[face : face + 1, :], (10, 256))

        exported = jnp.concatenate([sexp[0], dexp[...], jnp.zeros((2, 128), jnp.int32)], axis=0)
        nodex[...] = node_of(exported >> 8, faces)
        export_el = exported & 255
        export_cols = jnp.transpose(export_el)
        row_iota = lax.broadcasted_iota(jnp.int32, (256, 128), 0)
        lane_iota = lax.broadcasted_iota(jnp.int32, (128, 256), 1)
        for blk in range(BLOCKS):
            here = slice(128 * blk, 128 * blk + 128)
            ax[:, here] = one_hot(row_iota == export_el[blk : blk + 1])
            axt[here, :] = one_hot(lane_iota == export_cols[:, blk : blk + 1])

        def sub_copy(r, src, dst, send, recv_s, to, slot_from):
            return pltpu.make_async_remote_copy(
                src_ref=src.at[r, to],
                dst_ref=dst.at[r, slot_from],
                send_sem=send.at[r, to],
                recv_sem=recv_s.at[r, slot_from],
                device_id=(dom, to),
                device_id_type=MESH,
            )

        def dom_copy(r, src, dst, send, recv_s, block, slot, to):
            return pltpu.make_async_remote_copy(
                src_ref=src.at[r, block],
                dst_ref=dst.at[r, slot],
                send_sem=send.at[r, block],
                recv_sem=recv_s.at[r, slot],
                device_id=(to, sub),
                device_id_type=MESH,
            )

        has_low = dom > 0
        has_high = dom < DOMS - 1

        def start_all(r, src, dst, send, recv_s):
            for step in range(1, SUBS):
                to = lax.rem(sub + step, SUBS)
                sub_copy(r, src, dst, send, recv_s, to, sub).start()

            @pl.when(has_low)
            def _():
                dom_copy(r, src, dst, send, recv_s, 4, 5, dom - 1).start()

            @pl.when(has_high)
            def _():
                dom_copy(r, src, dst, send, recv_s, 5, 4, dom + 1).start()

        def wait_recv_all(r, src, dst, send, recv_s):
            for step in range(1, SUBS):
                other = lax.rem(sub + step, SUBS)
                sub_copy(r, src, dst, send, recv_s, other, other).wait_recv()

            @pl.when(has_low)
            def _():
                dom_copy(r, src, dst, send, recv_s, 4, 4, dom - 1).wait_recv()

            @pl.when(has_high)
            def _():
                dom_copy(r, src, dst, send, recv_s, 5, 5, dom + 1).wait_recv()

        def wait_send_all(r, src, dst, send, recv_s):
            for step in range(1, SUBS):
                to = lax.rem(sub + step, SUBS)
                sub_copy(r, src, dst, send, recv_s, to, sub).wait_send()

            @pl.when(has_low)
            def _():
                dom_copy(r, src, dst, send, recv_s, 4, 5, dom - 1).wait_send()

            @pl.when(has_high)
            def _():
                dom_copy(r, src, dst, send, recv_s, 5, 4, dom + 1).wait_send()

        fwd = (sf, rf, fs_sem, fr_sem)
        bwd = (sb, rb, bs_sem, br_sem)

        node_iota = lax.broadcasted_iota(jnp.int32, (ROWS, 128), 0)
        node_iota2 = lax.broadcasted_iota(jnp.int32, (ROWS, 256), 0)
        own_rows = node_iota2 < NODES

        def fold_pool():
            values = pool[...].reshape(6 * ROWS, 256)
            high = values.astype(bf16)
            pp[0:144, :] = high
            pp[144:288, :] = (values - high.astype(f32)).astype(bf16)

        def exports(r):
            for c in range(6):
                pool[c] = y[r, c]
            fold_pool()
            for blk in range(BLOCKS):
                got = dot(pp[...], ax[:, 128 * blk : 128 * blk + 128])
                got = got[:144] + got[144:]
                keep = node_iota == nodex[blk : blk + 1, :]
                for c in range(6):
                    sf[r, blk, c : c + 1, :] = jnp.sum(
                        jnp.where(keep, got[24 * c : 24 * c + 24], 0.0), axis=0, keepdims=True
                    )
            start_all(r, *fwd)

        def flux_rows(src, at):
            here = slice(at, at + 8)
            n = [nrm[i, here, :] for i in range(3)]
            e = [src[i, here, :] for i in range(3)]
            h = [src[3 + i, here, :] for i in range(3)]
            ne = n[0] * e[0] + n[1] * e[1] + n[2] * e[2]
            nh = n[0] * h[0] + n[1] * h[1] + n[2] * h[2]
            result = []
            for i in range(3):
                j, l = (i + 1) % 3, (i + 2) % 3
                result.append(n[i] * ne - e[i] - (n[j] * h[l] - n[l] * h[j]))
            for i in range(3):
                j, l = (i + 1) % 3, (i + 2) % 3
                result.append((n[j] * e[l] - n[l] * e[j]) + n[i] * nh - h[i])
            return result

        def curl_rows(e, h):
            for d in range(3):
                m = [met[3 * d + i : 3 * d + i + 1, :] for i in range(3)]
                here = slice(40 + 24 * d, 64 + 24 * d)
                for i in range(3):
                    j, l = (i + 1) % 3, (i + 2) % 3
                    x[i, here, :] = m[j] * h[l] - m[l] * h[j]
                    x[3 + i, here, :] = m[l] * e[j] - m[j] * e[l]

        def contracted(first, c):
            got = dot(tab[first : first + 48, 0:224], stacked(x[c]))
            return got[:24] + got[24:]

        def back_faces(r):
            for c in range(6):
                value = w[r, c]
                if c < 3:
                    value = value * ie
                got = dot(tab[96:176, 0:48], stacked(value))
                p[c] = (got[:40] + got[40:]) * scl[...]
            for at in range(0, FACE, 8):
                for c, value in enumerate(flux_rows(p, at)):
                    cd[c, at : at + 8, :] = value

            def group(g, carry):
                for j in range(8):
                    fn = g * 8 + j
                    keep = node_iota2 == nodes[pl.ds(fn, 1), :]
                    high, low = [], []
                    for c in range(6):
                        value = cd[c, pl.ds(fn, 1), :]
                        top = value.astype(bf16).astype(f32)
                        high.append(jnp.where(keep, top, 0.0))
                        low.append(jnp.where(keep, value - top, 0.0))
                    b_mat[:, 256 * j : 256 * j + 256] = jnp.concatenate(high + low, 0).astype(bf16)
                got = dot(b_mat[...], at_mat[pl.ds(pl.multiple_of(g * 2048, 2048), 2048), :])
                s_ref[...] = s_ref[...] - (got[:144] + got[144:])
                return carry

            s_ref[...] = jnp.zeros_like(s_ref)
            lax.fori_loop(0, FACE // 8, group, 0)
            for c in range(6):
                rows = s_ref[24 * c + 20 : 24 * c + 24, :]
                for blk in range(4):
                    at = 128 * (blk % 2)
                    sb[r, blk, c : c + 1, :] = rows[blk // 2 : blk // 2 + 1, at : at + 128]
                sb[r, 4, c : c + 1, :] = rows[2:3, 0:128]
                sb[r, 5, c : c + 1, :] = rows[3:4, 128:256]
            start_all(r, *bwd)

        def arrived(r, blk, dst, src):
            value = dst[r, blk]
            if blk < SUBS:
                value = jnp.where(sub == blk, src[r, blk], value)
            return value

        def forward(r):
            wait_recv_all(r, *fwd)
            for blk in range(4):
                value = arrived(r, blk, rf, sf)
                at = 128 * (blk % 2)
                for c in range(6):
                    row = 20 + blk // 2
                    pool[c, row : row + 1, at : at + 128] = value[c : c + 1]
            low, high = rf[r, 4], rf[r, 5]
            for c in range(6):
                pool[c, 22:23, 0:128] = low[c : c + 1]
                pool[c, 23:24, 128:256] = high[c : c + 1]
            fold_pool()

            def group(g, carry):
                for j in range(8):
                    fn = g * 8 + j
                    keep = node_iota2 == nodes[pl.ds(fn, 1), :]
                    got = dot(pp[...], a_mat[fn])
                    got = got[:144] + got[144:]
                    for c in range(6):
                        nb[c, pl.ds(fn, 1), :] = jnp.sum(
                            jnp.where(keep, got[24 * c : 24 * c + 24], 0.0), axis=0, keepdims=True
                        )
                return carry

            lax.fori_loop(0, FACE // 8, group, 0)
            for c in range(6):
                p[c] = dot(tab[176:216, 0:48], stacked(y[r, c])) - nb[c]
            for at in range(0, FACE, 8):
                factor = scl[at : at + 8, :]
                for c, value in enumerate(flux_rows(p, at)):
                    x[c, at : at + 8, :] = value * factor
            curl_rows([y[r, c] for c in range(3)], [y[r, 3 + c] for c in range(3)])
            for c in range(3):
                current = (ed * y[r, c] - y[r, 6 + c]) * it
                k[r, 6 + c] = current
                k[r, c] = (contracted(0, c) - current) * ie
                k[r, 3 + c] = contracted(0, 3 + c)

        def back_volume(r):
            for c in range(6):
                x[c, 0:40, :] = cd[c]
            curl_rows([w[r, c] * ie for c in range(3)], [w[r, 3 + c] for c in range(3)])
            wait_recv_all(r, *bwd)
            for blk in range(BLOCKS):
                value = arrived(r, blk, rb, sb)
                keep = node_iota == nodex[blk : blk + 1, :]
                top = value.astype(bf16).astype(f32)
                rest = value - top
                high = [jnp.where(keep, top[c : c + 1], 0.0) for c in range(6)]
                low = [jnp.where(keep, rest[c : c + 1], 0.0) for c in range(6)]
                bx[:, 128 * blk : 128 * blk + 128] = jnp.concatenate(high + low, 0).astype(bf16)
            got = dot(bx[...], axt[...])
            s_ref[...] = s_ref[...] + (got[:144] + got[144:])
            cots = []
            for c in range(6):
                value = contracted(48, c) + s_ref[24 * c : 24 * c + 24, :]
                cots.append(jnp.where(own_rows, value, 0.0))
            for c in range(3):
                through = (w[r, 6 + c] - w[r, c] * ie) * it
                cots[c] = cots[c] + ed * through
                cots.append(-through)
            return cots

        def one_round(r, ahead, adj_part, back_part):
            back_faces(r)
            forward(r)
            for c in range(9):
                y[r + 1, c] = y[0, c] + ahead * k[r, c]
            exports(r + 1)
            for c, value in enumerate(back_volume(r)):
                acc[c] = acc[c] + value
                w[r + 1, c] = adj_part * adj24[c] + back_part * value

        pl.semaphore_wait(barrier, SUBS - 1 + DOMS - 1)
        exports(0)
        index = nbr[...]
        nodes[...] = node_of(index >> 8, faces)
        element = index & 255
        columns = jnp.transpose(element)
        lane_iota2 = lax.broadcasted_iota(jnp.int32, (256, 256), 1)
        row_iota2 = lax.broadcasted_iota(jnp.int32, (256, 256), 0)
        for fn in range(FACE):
            at_mat[256 * fn : 256 * fn + 256, :] = one_hot(lane_iota2 == columns[:, fn : fn + 1])
            a_mat[fn] = one_hot(row_iota2 == element[fn : fn + 1])

        def looped(r, carry):
            last = r == 2
            one_round(
                r,
                jnp.where(last, time_step, 0.5 * time_step),
                jnp.where(last, time_step / 6.0, time_step / 3.0),
                jnp.where(r == 0, time_step, 0.5 * time_step),
            )
            return carry

        lax.fori_loop(0, 3, looped, 0)
        back_faces(3)
        forward(3)

        sums = [jnp.zeros((ROWS, 256), f32) for _ in range(3)]
        for r in range(4):
            for c in range(3):
                through = w[3 - r, 6 + c] - w[3 - r, c] * ie
                sums[0] = sums[0] - w[3 - r, c] * k[r, c]
                sums[1] = sums[1] + through * y[r, c]
                sums[2] = sums[2] - through * k[r, 6 + c]
        grads = [
            jnp.sum(value, axis=0, keepdims=True) * factor
            for value, factor in zip(sums, (ie, it, it))
        ]
        slot = sslot[...]
        target = ((slot >> 1) & 3) * DOMS + (slot >> 3)
        chosen = one_hot(lax.broadcasted_iota(jnp.int32, (128, 256), 0) == target)
        lines = [jnp.where((slot & 1) == q, g, 0.0) for q in range(2) for g in grads]
        lines = jnp.concatenate(lines + [jnp.zeros((2, 256), f32)], axis=0)
        lines = [jnp.where(sub == q, lines, 0.0) for q in range(SUBS)]
        lines = jnp.concatenate(lines + [jnp.zeros((96, 256), f32)], axis=0)
        packed = sum(dot(chosen, part) for part in parts3(jnp.transpose(lines)))
        for q in range(SUBS):
            ya[q] = packed[DOMS * q : DOMS * q + DOMS]

        def first_hop(to, slot_from):
            return pltpu.make_async_remote_copy(
                src_ref=ya.at[to],
                dst_ref=yr.at[slot_from],
                send_sem=ps_sem.at[to],
                recv_sem=pr_sem.at[slot_from],
                device_id=(dom, to),
                device_id_type=MESH,
            )

        for step in range(1, SUBS):
            first_hop(lax.rem(sub + step, SUBS), sub).start()
        for step in range(1, SUBS):
            other = lax.rem(sub + step, SUBS)
            first_hop(other, other).wait_recv()
        mine = ya[pl.ds(sub, 1)][0] + yr[0] + yr[1] + yr[2] + yr[3]
        for q in range(DOMS):
            cb[q] = mine[q : q + 1]

        def second_hop(to, slot_from):
            return pltpu.make_async_remote_copy(
                src_ref=cb.at[to],
                dst_ref=rc.at[slot_from],
                send_sem=qs_sem.at[to],
                recv_sem=qr_sem.at[slot_from],
                device_id=(to, sub),
                device_id_type=MESH,
            )

        def hop_start(step, carry):
            second_hop(lax.rem(dom + step, DOMS), dom).start()
            return carry

        def hop_wait(step, carry):
            other = lax.rem(dom + step, DOMS)
            second_hop(other, other).wait_recv()
            return carry

        def hop_sent(step, carry):
            second_hop(lax.rem(dom + step, DOMS), dom).wait_send()
            return carry

        lax.fori_loop(1, DOMS, hop_start, 0)

        for c, value in enumerate(back_volume(3)):
            out[c] = (acc[c] + value)[:NODES]

        lax.fori_loop(1, DOMS, hop_wait, 0)
        here = lax.broadcasted_iota(jnp.int32, (DOMS, 128), 0) == dom
        came = jnp.concatenate([rc[q] for q in range(DOMS)], axis=0)
        came = came + jnp.where(here, mine, 0.0)
        turned = parts3(jnp.transpose(came)[:32])
        lanes = lax.broadcasted_iota(jnp.int32, (DOMS, 128), 1)
        total = jnp.zeros((3, 128), f32)
        for q in range(SUBS):
            ids = recv[:, 2 * q : 2 * q + 2]
            for z in range(2):
                owner = one_hot(lanes == ids[:, z : z + 1])
                at = 8 * q + 3 * z
                for part in turned:
                    total = total + dot(part, owner)[at : at + 3]
        therm[...] = total[:, :64]

        for r in range(4):
            wait_send_all(r, *fwd)
            wait_send_all(r, *bwd)
        for step in range(1, SUBS):
            first_hop(lax.rem(sub + step, SUBS), sub).wait_send()
        lax.fori_loop(1, DOMS, hop_sent, 0)

    return kernel


def per_device(
    field_state,
    adjoint,
    eps_inf,
    eps_delta,
    relax_time,
    metric,
    face_scale,
    face_angles,
    nbr_index,
    dom_export,
    sub_export,
    send_slot,
    recv_index,
):
    table, faces = host_tables()
    stage = pltpu.VMEM((4, 9, ROWS, 256), f32)
    trace = pltpu.VMEM((6, FACE, 256), f32)
    message = pltpu.VMEM((4, BLOCKS, 8, 128), f32)
    semaphores = pltpu.SemaphoreType.DMA((4, BLOCKS))
    state = pltpu.VMEM((9, ROWS, 256), f32)
    scratch = [
        stage, stage, stage, state, state,
        pltpu.VMEM((3, FACE, 256), f32),
        pltpu.VMEM((FACE, 256), f32),
        pltpu.VMEM((6, 112, 256), f32),
        trace, trace, trace,
        pltpu.VMEM((6 * ROWS, 256), f32),
        pltpu.VMEM((6, ROWS, 256), f32),
        pltpu.VMEM((12 * ROWS, 256), bf16),
        pltpu.VMEM((FACE, 256), jnp.int32),
        pltpu.VMEM((8, 128), jnp.int32),
        pltpu.VMEM((FACE, 256, 256), bf16),
        pltpu.VMEM((FACE * 256, 256), bf16),
        pltpu.VMEM((256, 128 * BLOCKS), bf16),
        pltpu.VMEM((128 * BLOCKS, 256), bf16),
        pltpu.VMEM((12 * ROWS, 2048), bf16),
        pltpu.VMEM((12 * ROWS, 128 * BLOCKS), bf16),
        message, message, message, message,
        pltpu.VMEM((SUBS, DOMS, 128), f32),
        pltpu.VMEM((SUBS, DOMS, 128), f32),
        pltpu.VMEM((DOMS, 1, 128), f32),
        pltpu.VMEM((DOMS, 1, 128), f32),
        semaphores, semaphores, semaphores, semaphores,
        pltpu.SemaphoreType.DMA((SUBS,)),
        pltpu.SemaphoreType.DMA((SUBS,)),
        pltpu.SemaphoreType.DMA((DOMS,)),
        pltpu.SemaphoreType.DMA((DOMS,)),
    ]
    call = pl.pallas_call(
        kernel_of(faces),
        out_shape=(
            jax.ShapeDtypeStruct((9, NODES, 256), f32),
            jax.ShapeDtypeStruct((3, 64), f32),
        ),
        in_specs=[pl.BlockSpec(memory_space=pltpu.VMEM)] * 14,
        out_specs=(
            pl.BlockSpec(memory_space=pltpu.VMEM),
            pl.BlockSpec(memory_space=pltpu.VMEM),
        ),
        scratch_shapes=scratch,
        compiler_params=pltpu.CompilerParams(
            collective_id=0, has_side_effects=True, vmem_limit_bytes=48 << 20
        ),
        name="reverse_step",
    )
    return call(
        field_state,
        adjoint,
        eps_inf.reshape(1, 256),
        eps_delta.reshape(1, 256),
        relax_time.reshape(1, 256),
        metric,
        face_scale,
        face_angles,
        nbr_index,
        dom_export.reshape(2, 128),
        sub_export,
        send_slot.reshape(1, 256),
        recv_index.reshape(32, 8),
        jnp.asarray(table),
    )


def solution(mesh):
    both = ("dom", "sub")
    return jax.shard_map(
        per_device,
        mesh=mesh,
        in_specs=(
            P(None, None, both),
            P(None, None, both),
            P(both),
            P(both),
            P(both),
            P(None, both),
            P(None, both),
            P(None, None, both),
            P(None, both),
            P(both),
            P(both, None, None),
            P(both),
            P(both, None, None),
        ),
        out_specs=(P(None, None, both), P(None, both)),
        check_vma=False,
    )
```

time: 1030 us -> 60.3 us (0.06)
  local copies, waits for them, and re-layouts: 404 us -> 10.2 us
  other arithmetic: 365 us -> 0 us
  matrix products: 81.7 us -> 0 us
  starting transfers between devices: 68.6 us -> 0 us
  waiting for transfers between devices: 51.5 us -> 0 us
  Pallas kernels: 0 us -> 48.9 us
  blocking collectives: 38 us -> 0 us
  between operations: 16.6 us -> 0.68 us
    scatter-add x26 -> x0, other arithmetic: 304 us -> none  [the longest x4 232 us: local_part(): neighbour = pool[:, flat_index].reshape(6, 40, elements)]
    gather x24 -> x0, local copies, waits for them, and re-layouts: 181 us -> none  [the longest x4 149 us: local_part(): neighbour = pool[:, flat_index].reshape(6, 40, elements)]
    dot_general x24 -> x0, matrix products: 81.7 us -> none  [the longest x8 63.6 us: element_rhs(): jnp.einsum('dik,dcnk->icnk', metric.reshape(3, 3, elements), derived, pre...]
    slice x29 -> x0, local copies, waits for them, and re-layouts: 70.7 us -> none  [the longest x8 48.4 us: element_rhs(): jump_e = traces[0:3] - neighbour[0:3]]
    ppermute x16 -> x0, starting transfers between devices: 59.6 us -> none  [the longest x8 44.3 us: extended(): lax.ppermute(lax.slice_in_dim(block, block.shape[dim] - width, None, axis...]
    reshape x19 -> x1, local copies, waits for them, and re-layouts: 52.7 us -> 0.08 us  [per_device(): recv_index.reshape(32, 8)]
    reduce_scatter x4 -> x0, waiting for transfers between devices: 49.7 us -> none  [sub_trade(): lax.psum_scatter(spread.reshape(6, sub_count * sub_count, sub_slots), 'su...]
    pallas_call x0 -> x1, Pallas kernels: none -> 48.9 us  [per_device(): call(field_state, adjoint, eps_inf.reshape(1, 256), eps_delta.reshape(1,...]
  transfers between devices with their start and end apart: 21 -> 0, of which waited for: 6 -> 0; matrix products, arithmetic and copies ran while one was open for 20% -> 0% of each run, Pallas kernels for 0% -> 0%
where the time goes in v1:
time: 60.3 us; the launch traced here: 59.8 us
  Pallas kernels  48.9 us (81%)
  local copies, waits for them, and re-layouts  10.2 us (17%)
  between operations  0.68 us (1%)
    pallas_call x1, Pallas kernels, per_device(): call(field_state, adjoint, eps_inf.reshape(1, 256), eps_delta.reshape(1,...  48.9 us
    unnamed x29, local copies, waits for them, and re-layouts  10.2 us

profile of v1, /device:TPU:1, one launch (start us, length us, event | category | flops | bytes accessed | tf_op | source)
XLA Modules:
  0.0 59.8 jit_solution(123543860437696474)
XLA Ops:
  0.6 0.0 copy-start.2
  0.6 0.8 %copy.17 = s32[1,128,2]{2,1,0:T(8,128)S(1)} copy(s32[1,128,2]{1,2,0:T(2,128)} %param.26) | data formatting | bytes 2048 | tf_op args[12]
  1.5 0.0 copy-start.3
  1.5 0.0 copy-start.7
  1.5 0.1 reshape.27.recv
  1.6 0.0 copy-done.2
  1.6 0.7 %copy-done.3 = s32[40,256]{1,0:T(8,128)S(1)} copy-done((s32[40,256]{1,0:T(8,128)S(1)}, s32[40,256]{1,0:T(8,128)}, u32[]{:S(2)}) %copy-start.3) | copy-done | bytes 40984
  2.3 0.0 copy-done.7
  2.3 0.0 copy-start
  2.3 0.9 %copy-done = f32[9,20,256]{2,1,0:T(8,128)S(1)} copy-done((f32[9,20,256]{2,1,0:T(8,128)S(1)}, f32[9,20,256]{2,1,0:T(8,128)}, u32[]{:S(2)}) %copy-start) | copy-done | bytes 184344
  3.2 0.0 copy-start.1
  3.2 0.9 %copy-done.1 = f32[9,20,256]{2,1,0:T(8,128)S(1)} copy-done((f32[9,20,256]{2,1,0:T(8,128)S(1)}, f32[9,20,256]{2,1,0:T(8,128)}, u32[]{:S(2)}) %copy-start.1) | copy-done | bytes 184344
  4.1 0.0 copy-start.4
  4.1 0.7 %copy-done.4 = f32[9,256]{1,0:T(8,128)S(1)} copy-done((f32[9,256]{1,0:T(8,128)S(1)}, f32[9,256]{1,0:T(8,128)}, u32[]{:S(2)}) %copy-start.4) | copy-done | bytes 9240
  4.8 0.0 copy-start.5
  4.9 0.7 %copy-done.5 = f32[2,4,256]{2,1,0:T(4,128)S(1)} copy-done((f32[2,4,256]{2,1,0:T(4,128)S(1)}, f32[2,4,256]{2,1,0:T(4,128)}, u32[]{:S(2)}) %copy-start.5) | copy-done | bytes 8216
  5.5 0.0 copy-start.6
  5.5 0.7 %copy-done.6 = f32[4,256]{1,0:T(4,128)S(1)} copy-done((f32[4,256]{1,0:T(4,128)S(1)}, f32[4,256]{1,0:T(4,128)}, u32[]{:S(2)}) %copy-start.6) | copy-done | bytes 4120
  6.2 0.0 copy-start.8
  6.2 0.7 %copy-done.8 = f32[256]{0:T(256)S(1)} copy-done((f32[256]{0:T(256)S(1)}, f32[256]{0:T(256)}, u32[]{:S(2)}) %copy-start.8) | copy-done | bytes 1048
  6.9 0.0 copy-start.9
  6.9 0.7 %copy-done.9 = f32[256]{0:T(256)S(1)} copy-done((f32[256]{0:T(256)S(1)}, f32[256]{0:T(256)}, u32[]{:S(2)}) %copy-start.9) | copy-done | bytes 1048
  7.6 0.0 copy-start.10
  7.6 0.7 %copy-done.10 = f32[256]{0:T(256)S(1)} copy-done((f32[256]{0:T(256)S(1)}, f32[256]{0:T(256)}, u32[]{:S(2)}) %copy-start.10) | copy-done | bytes 1048
  8.3 0.0 copy-start.11
  8.3 0.7 %copy-done.11 = s32[256]{0:T(256)S(1)} copy-done((s32[256]{0:T(256)S(1)}, s32[256]{0:T(256)}, u32[]{:S(2)}) %copy-start.11) | copy-done | bytes 1048
  9.0 0.0 copy-start.12
  9.0 0.7 %copy-done.12 = s32[256]{0:T(256)S(1)} copy-done((s32[256]{0:T(256)S(1)}, s32[256]{0:T(256)}, u32[]{:S(2)}) %copy-start.12) | copy-done | bytes 1048
  9.6 48.9 %reverse_step.1 = (f32[9,20,256]{2,1,0:T(8,128)S(1)}, f32[3,64]{1,0:T(4,128)S(1)}) custom-call(f32[9,20,256]{2,1,0:T(8,128)S(1)} %copy-done, f32[9,20,256]{2,1,0:T(8,128)S(1)} %copy-done.1, f32[1,256]{1,0:T(1,128)S(1)} %bitcast.5, f32[1,256]{1,0:T(1,128)S(1)} %bitcast.6, f32[1,256]{1,0:T(1,128)S(1)} %bitcast.7, f32[9,256]{1,0:T(8,128)S(1)} %copy-done.4, ...), custom_call_target="tpu_custom_call" | custom-call | tf_op jit(solution)/shard_map/reverse_step/pallas_call | solution.py:670
  58.6 0.7 %copy.20 = f32[9,20,256]{2,1,0:T(8,128)} copy(f32[9,20,256]{2,1,0:T(8,128)S(1)} %get-tuple-element.4) | data formatting | bytes 368640
  59.3 0.6 copy.21
Async XLA Ops:
  0.6 0.9 %copy-start.2 = (bf16[224,256]{1,0:T(8,128)(2,1)S(1)}, bf16[224,256]{1,0:T(8,128)(2,1)}, u32[]{:S(2)}) copy-start(bf16[224,256]{1,0:T(8,128)(2,1)} %constant.2.clone.tab) | copy-start | bytes 344068
  1.5 0.8 %copy-start.3 = (s32[40,256]{1,0:T(8,128)S(1)}, s32[40,256]{1,0:T(8,128)}, u32[]{:S(2)}) copy-start(s32[40,256]{1,0:T(8,128)} %nbr.1) | copy-start | bytes 122884
  1.5 0.8 %copy-start.7 = (s32[1,4,128]{2,1,0:T(4,128)S(1)}, s32[1,4,128]{2,1,0:T(4,128)}, u32[]{:S(2)}) copy-start(s32[1,4,128]{2,1,0:T(4,128)} %sexp.1) | copy-start | bytes 6148
  2.3 0.9 %copy-start = (f32[9,20,256]{2,1,0:T(8,128)S(1)}, f32[9,20,256]{2,1,0:T(8,128)}, u32[]{:S(2)}) copy-start(f32[9,20,256]{2,1,0:T(8,128)} %fs.1) | copy-start | bytes 552964
  3.2 0.9 %copy-start.1 = (f32[9,20,256]{2,1,0:T(8,128)S(1)}, f32[9,20,256]{2,1,0:T(8,128)}, u32[]{:S(2)}) copy-start(f32[9,20,256]{2,1,0:T(8,128)} %adj.1) | copy-start | bytes 552964
  4.1 0.7 %copy-start.4 = (f32[9,256]{1,0:T(8,128)S(1)}, f32[9,256]{1,0:T(8,128)}, u32[]{:S(2)}) copy-start(f32[9,256]{1,0:T(8,128)} %met.1) | copy-start | bytes 27652
  4.8 0.7 %copy-start.5 = (f32[2,4,256]{2,1,0:T(4,128)S(1)}, f32[2,4,256]{2,1,0:T(4,128)}, u32[]{:S(2)}) copy-start(f32[2,4,256]{2,1,0:T(4,128)} %ang.1) | copy-start | bytes 24580
  5.5 0.7 %copy-start.6 = (f32[4,256]{1,0:T(4,128)S(1)}, f32[4,256]{1,0:T(4,128)}, u32[]{:S(2)}) copy-start(f32[4,256]{1,0:T(4,128)} %fsc.1) | copy-start | bytes 12292
  6.2 0.7 %copy-start.8 = (f32[256]{0:T(256)S(1)}, f32[256]{0:T(256)}, u32[]{:S(2)}) copy-start(f32[256]{0:T(256)} %param.16) | copy-start | bytes 3076
  6.9 0.7 %copy-start.9 = (f32[256]{0:T(256)S(1)}, f32[256]{0:T(256)}, u32[]{:S(2)}) copy-start(f32[256]{0:T(256)} %param.17) | copy-start | bytes 3076
  7.6 0.7 %copy-start.10 = (f32[256]{0:T(256)S(1)}, f32[256]{0:T(256)}, u32[]{:S(2)}) copy-start(f32[256]{0:T(256)} %param.18) | copy-start | bytes 3076
  8.3 0.7 %copy-start.11 = (s32[256]{0:T(256)S(1)}, s32[256]{0:T(256)}, u32[]{:S(2)}) copy-start(s32[256]{0:T(256)} %param.23) | copy-start | bytes 3076
  9.0 0.7 %copy-start.12 = (s32[256]{0:T(256)S(1)}, s32[256]{0:T(256)}, u32[]{:S(2)}) copy-start(s32[256]{0:T(256)} %param.25) | copy-start | bytes 3076

commit v2 on v1

--- a/solution.py
+++ b/solution.py
@@ -187,13 +187,26 @@
 
 def kernel_of(faces):
     def kernel(
-        fs, adj, einf, edel, tau, met, fsc, ang, nbr, dexp, sexp, sslot, recv, tab,
-        out, therm,
+        *refs,
+    ):
+        given, refs = refs[:14], refs[14:]
+        out, therm = refs[:2]
+        held, in_sem, refs = refs[2:16], refs[16], refs[17:]
+        fs, adj, einf, edel, tau, met, fsc, ang, nbr, dexp, sexp, sslot, recv, tab = held
+        (
         y, k, w, adj24, acc, nrm, scl, x, p, nb, cd, s_ref, pool, pp, nodes, nodex,
-        a_mat, at_mat, ax, axt, b_mat, bx,
+        a_mat, at_mat, ax, axt, b_mat, bx, oids, oh,
         sf, rf, sb, rb, ya, yr, cb, rc,
         fs_sem, fr_sem, bs_sem, br_sem, ps_sem, pr_sem, qs_sem, qr_sem,
-    ):
+        ) = refs
+
+        def fetch(i):
+            return pltpu.make_async_copy(given[i], held[i], in_sem.at[i])
+
+        order = (10, 9, 0, 13, 8, 1, 2, 4, 3, 7, 6, 5, 11, 12)
+        for i in order:
+            fetch(i).start()
+
         dom = lax.axis_index("dom")
         sub = lax.axis_index("sub")
 
@@ -215,6 +228,8 @@
 
         lax.fori_loop(1, DOMS, greet, 0)
 
+        for i in order:
+            fetch(i).wait()
         ie = 1.0 / einf[...]
         it = 1.0 / tau[...]
         ed = edel[...]
@@ -492,6 +507,15 @@
             at_mat[256 * fn : 256 * fn + 256, :] = one_hot(lane_iota2 == columns[:, fn : fn + 1])
             a_mat[fn] = one_hot(row_iota2 == element[fn : fn + 1])
 
+        owners = jnp.transpose(jnp.concatenate([recv[0], jnp.zeros((6, 128), jnp.int32)], axis=0))
+        oids[...] = owners
+        lanes = lax.broadcasted_iota(jnp.int32, (DOMS, 128), 1)
+        for q in range(SUBS):
+            ids = oids[pl.ds(q, DOMS, stride=SUBS), :]
+            for z in range(2):
+                at = 128 * (2 * q + z)
+                oh[:, at : at + 128] = one_hot(lanes == ids[:, z : z + 1])
+
         def looped(r, carry):
             last = r == 2
             one_round(
@@ -579,16 +603,14 @@
         here = lax.broadcasted_iota(jnp.int32, (DOMS, 128), 0) == dom
         came = jnp.concatenate([rc[q] for q in range(DOMS)], axis=0)
         came = came + jnp.where(here, mine, 0.0)
-        turned = parts3(jnp.transpose(came)[:32])
-        lanes = lax.broadcasted_iota(jnp.int32, (DOMS, 128), 1)
+        turned = jnp.concatenate(parts3(jnp.transpose(came)[:32]), axis=0)
+        spread = dot(turned, oh[...])
+        spread = spread[:32] + spread[32:64] + spread[64:]
         total = jnp.zeros((3, 128), f32)
         for q in range(SUBS):
-            ids = recv[:, 2 * q : 2 * q + 2]
             for z in range(2):
-                owner = one_hot(lanes == ids[:, z : z + 1])
-                at = 8 * q + 3 * z
-                for part in turned:
-                    total = total + dot(part, owner)[at : at + 3]
+                row, at = 8 * q + 3 * z, 128 * (2 * q + z)
+                total = total + spread[row : row + 3, at : at + 128]
         therm[...] = total[:, :64]
 
         for r in range(4):
@@ -622,7 +644,24 @@
     message = pltpu.VMEM((4, BLOCKS, 8, 128), f32)
     semaphores = pltpu.SemaphoreType.DMA((4, BLOCKS))
     state = pltpu.VMEM((9, ROWS, 256), f32)
-    scratch = [
+    values = (
+        field_state,
+        adjoint,
+        eps_inf.reshape(1, 256),
+        eps_delta.reshape(1, 256),
+        relax_time.reshape(1, 256),
+        metric,
+        face_scale,
+        face_angles,
+        nbr_index,
+        dom_export.reshape(2, 128),
+        sub_export,
+        send_slot.reshape(1, 256),
+        jnp.transpose(recv_index, (0, 2, 1)),
+        jnp.asarray(table),
+    )
+    scratch = [pltpu.VMEM(value.shape, value.dtype) for value in values] + [
+        pltpu.SemaphoreType.DMA((len(values),)),
         stage, stage, stage, state, state,
         pltpu.VMEM((3, FACE, 256), f32),
         pltpu.VMEM((FACE, 256), f32),
@@ -639,6 +678,8 @@
         pltpu.VMEM((128 * BLOCKS, 256), bf16),
         pltpu.VMEM((12 * ROWS, 2048), bf16),
         pltpu.VMEM((12 * ROWS, 128 * BLOCKS), bf16),
+        pltpu.VMEM((128, 8), jnp.int32),
+        pltpu.VMEM((DOMS, 1024), bf16),
         message, message, message, message,
         pltpu.VMEM((SUBS, DOMS, 128), f32),
         pltpu.VMEM((SUBS, DOMS, 128), f32),
@@ -656,33 +697,18 @@
             jax.ShapeDtypeStruct((9, NODES, 256), f32),
             jax.ShapeDtypeStruct((3, 64), f32),
         ),
-        in_specs=[pl.BlockSpec(memory_space=pltpu.VMEM)] * 14,
+        in_specs=[pl.BlockSpec(memory_space=pltpu.HBM)] * 14,
         out_specs=(
             pl.BlockSpec(memory_space=pltpu.VMEM),
             pl.BlockSpec(memory_space=pltpu.VMEM),
         ),
         scratch_shapes=scratch,
         compiler_params=pltpu.CompilerParams(
-            collective_id=0, has_side_effects=True, vmem_limit_bytes=48 << 20
+            collective_id=0, has_side_effects=True, vmem_limit_bytes=32 << 20
         ),
         name="reverse_step",
     )
-    return call(
-        field_state,
-        adjoint,
-        eps_inf.reshape(1, 256),
-        eps_delta.reshape(1, 256),
-        relax_time.reshape(1, 256),
-        metric,
-        face_scale,
-        face_angles,
-        nbr_index,
-        dom_export.reshape(2, 128),
-        sub_export,
-        send_slot.reshape(1, 256),
-        recv_index.reshape(32, 8),
-        jnp.asarray(table),
-    )
+    return call(*[pltpu.with_memory_space_constraint(v, pltpu.HBM) for v in values])
 
 
 def solution(mesh):

time: 60.3 us -> 51.2 us (0.85)
  local copies, waits for them, and re-layouts: 10.2 us -> 1.27 us
    unnamed x29 -> x2, local copies, waits for them, and re-layouts: 10.2 us -> 1.27 us
where the time goes in v2:
time: 51.2 us; the launch traced here: 51 us
  Pallas kernels  49.1 us (96%)
  local copies, waits for them, and re-layouts  1.27 us (2%)
  between operations  0.64 us (1%)
    pallas_call x1, Pallas kernels, per_device(): call(*[pltpu.with_memory_space_constraint(v, pltpu.HBM) for v in values])  49.1 us
    unnamed x2, local copies, waits for them, and re-layouts  1.27 us

profile of v2, /device:TPU:1, one launch (start us, length us, event | category | flops | bytes accessed | tf_op | source)
XLA Modules:
  0.0 51.0 jit_solution(13289831316293138074)
XLA Ops:
  0.6 49.1 %reverse_step.1 = (f32[9,20,256]{2,1,0:T(8,128)S(1)}, f32[3,64]{1,0:T(4,128)S(1)}) custom-call(f32[9,20,256]{2,1,0:T(8,128)} %refs_0_.1, f32[9,20,256]{2,1,0:T(8,128)} %refs_1_.1, f32[1,256]{1,0:T(1,128)} %bitcast.6, f32[1,256]{1,0:T(1,128)} %bitcast.7, f32[1,256]{1,0:T(1,128)} %bitcast.8, f32[9,256]{1,0:T(8,128)} %refs_5_.1, f32[4,256]{1,0:T(4,128)} %refs_6_.1, ...), custom_call_target="tpu_custom_call" | custom-call | tf_op jit(solution)/shard_map/reverse_step/pallas_call | solution.py:711
  49.8 0.7 %copy.18 = f32[9,20,256]{2,1,0:T(8,128)} copy(f32[9,20,256]{2,1,0:T(8,128)S(1)} %get-tuple-element.4) | data formatting | bytes 368640
  50.5 0.6 %copy.19 = f32[3,64]{1,0:T(4,128)} copy(f32[3,64]{1,0:T(4,128)S(1)} %get-tuple-element.5) | data formatting | bytes 1536

commit v3 on v2

--- a/solution.py
+++ b/solution.py
@@ -17,6 +17,9 @@
 DOMS = 32
 SUBS = 4
 BLOCKS = 6
+SEATS = 8
+SITES = 16
+GROUP = 8
 MESH = pl.DeviceIdType.MESH
 
 
@@ -194,7 +197,7 @@
         held, in_sem, refs = refs[2:16], refs[16], refs[17:]
         fs, adj, einf, edel, tau, met, fsc, ang, nbr, dexp, sexp, sslot, recv, tab = held
         (
-        y, k, w, adj24, acc, nrm, scl, x, p, nb, cd, s_ref, pool, pp, nodes, nodex,
+        y, k, w, adj24, acc, nrm, scl, x, xb, p, nb, cd, s_ref, pool, pp, nodes, nodex,
         a_mat, at_mat, ax, axt, b_mat, bx, oids, oh,
         sf, rf, sb, rb, ya, yr, cb, rc,
         fs_sem, fr_sem, bs_sem, br_sem, ps_sem, pr_sem, qs_sem, qr_sem,
@@ -215,18 +218,37 @@
         yr[...] = jnp.zeros_like(yr)
         rc[...] = jnp.zeros_like(rc)
         barrier = pltpu.get_barrier_semaphore()
-        for step in range(1, SUBS):
-            pl.semaphore_signal(
-                barrier, inc=1, device_id=(dom, lax.rem(sub + step, SUBS)), device_id_type=MESH
-            )
-
-        def greet(step, carry):
-            pl.semaphore_signal(
-                barrier, inc=1, device_id=(lax.rem(dom + step, DOMS), sub), device_id_type=MESH
-            )
-            return carry
-
-        lax.fori_loop(1, DOMS, greet, 0)
+        core = lax.rem(dom, 2)
+        site = dom // 2
+        seat = sub * 2 + core
+
+        def seat_device(other):
+            return (site * 2 + lax.rem(other, 2), other // 2)
+
+        def site_device(other):
+            return (other * 2 + core, sub)
+
+        def greet(device):
+            pl.semaphore_signal(barrier, inc=1, device_id=device, device_id_type=MESH)
+
+        for step in range(1, SEATS):
+            greet(seat_device(lax.rem(seat + step, SEATS)))
+        for step in range(1, SITES):
+            greet(site_device(lax.rem(site + step, SITES)))
+        has_low = dom > 0
+        has_high = dom < DOMS - 1
+
+        @pl.when(has_low & (core == 0))
+        def _():
+            greet((dom - 1, sub))
+
+        @pl.when(has_high & (core == 1))
+        def _():
+            greet((dom + 1, sub))
+
+        def meet():
+            outside = (has_low & (core == 0)) | (has_high & (core == 1))
+            pl.semaphore_wait(barrier, jnp.where(outside, SEATS + SITES - 1, SEATS + SITES - 2))
 
         for i in order:
             fetch(i).wait()
@@ -279,9 +301,6 @@
                 device_id_type=MESH,
             )
 
-        has_low = dom > 0
-        has_high = dom < DOMS - 1
-
         def start_all(r, src, dst, send, recv_s):
             for step in range(1, SUBS):
                 to = lax.rem(sub + step, SUBS)
@@ -338,16 +357,17 @@
             for c in range(6):
                 pool[c] = y[r, c]
             fold_pool()
-            for blk in range(BLOCKS):
-                got = dot(pp[...], ax[:, 128 * blk : 128 * blk + 128])
-                got = got[:144] + got[144:]
-                keep = node_iota == nodex[blk : blk + 1, :]
-                for c in range(6):
-                    sf[r, blk, c : c + 1, :] = jnp.sum(
-                        jnp.where(keep, got[24 * c : 24 * c + 24], 0.0), axis=0, keepdims=True
-                    )
-            start_all(r, *fwd)
-
+            for pair in range(BLOCKS // 2):
+                both = dot(pp[...], ax[:, 256 * pair : 256 * pair + 256])
+                both = both[:144] + both[144:]
+                for half in range(2):
+                    blk = 2 * pair + half
+                    got = both[:, 128 * half : 128 * half + 128]
+                    keep = node_iota == nodex[blk : blk + 1, :]
+                    for c in range(6):
+                        sf[r, blk, c : c + 1, :] = jnp.sum(
+                            jnp.where(keep, got[24 * c : 24 * c + 24], 0.0), axis=0, keepdims=True
+                        )
         def flux_rows(src, at):
             here = slice(at, at + 8)
             n = [nrm[i, here, :] for i in range(3)]
@@ -364,7 +384,7 @@
                 result.append((n[j] * e[l] - n[l] * e[j]) + n[i] * nh - h[i])
             return result
 
-        def curl_rows(e, h):
+        def curl_rows(x, e, h):
             for d in range(3):
                 m = [met[3 * d + i : 3 * d + i + 1, :] for i in range(3)]
                 here = slice(40 + 24 * d, 64 + 24 * d)
@@ -373,11 +393,11 @@
                     x[i, here, :] = m[j] * h[l] - m[l] * h[j]
                     x[3 + i, here, :] = m[l] * e[j] - m[j] * e[l]
 
-        def contracted(first, c):
+        def contracted(x, first, c):
             got = dot(tab[first : first + 48, 0:224], stacked(x[c]))
             return got[:24] + got[24:]
 
-        def back_faces(r):
+        def back_flux(r):
             for c in range(6):
                 value = w[r, c]
                 if c < 3:
@@ -388,23 +408,41 @@
                 for c, value in enumerate(flux_rows(p, at)):
                     cd[c, at : at + 8, :] = value
 
+        def sweep(gather, scatter):
             def group(g, carry):
-                for j in range(8):
-                    fn = g * 8 + j
+                for j in range(GROUP):
+                    fn = g * GROUP + j
                     keep = node_iota2 == nodes[pl.ds(fn, 1), :]
-                    high, low = [], []
-                    for c in range(6):
-                        value = cd[c, pl.ds(fn, 1), :]
-                        top = value.astype(bf16).astype(f32)
-                        high.append(jnp.where(keep, top, 0.0))
-                        low.append(jnp.where(keep, value - top, 0.0))
-                    b_mat[:, 256 * j : 256 * j + 256] = jnp.concatenate(high + low, 0).astype(bf16)
-                got = dot(b_mat[...], at_mat[pl.ds(pl.multiple_of(g * 2048, 2048), 2048), :])
-                s_ref[...] = s_ref[...] - (got[:144] + got[144:])
+                    if gather:
+                        got = dot(pp[...], a_mat[fn])
+                        got = got[:144] + got[144:]
+                        for c in range(6):
+                            nb[c, pl.ds(fn, 1), :] = jnp.sum(
+                                jnp.where(keep, got[24 * c : 24 * c + 24], 0.0),
+                                axis=0,
+                                keepdims=True,
+                            )
+                    if scatter:
+                        high, low = [], []
+                        for c in range(6):
+                            value = cd[c, pl.ds(fn, 1), :]
+                            top = value.astype(bf16).astype(f32)
+                            high.append(jnp.where(keep, top, 0.0))
+                            low.append(jnp.where(keep, value - top, 0.0))
+                        b_mat[:, 256 * j : 256 * j + 256] = jnp.concatenate(high + low, 0).astype(
+                            bf16
+                        )
+                if scatter:
+                    span = GROUP * 256
+                    got = dot(b_mat[...], at_mat[pl.ds(pl.multiple_of(g * span, span), span), :])
+                    s_ref[...] = s_ref[...] - (got[:144] + got[144:])
                 return carry
 
-            s_ref[...] = jnp.zeros_like(s_ref)
-            lax.fori_loop(0, FACE // 8, group, 0)
+            if scatter:
+                s_ref[...] = jnp.zeros_like(s_ref)
+            lax.fori_loop(0, FACE // GROUP, group, 0)
+
+        def give_back(r):
             for c in range(6):
                 rows = s_ref[24 * c + 20 : 24 * c + 24, :]
                 for blk in range(4):
@@ -412,7 +450,6 @@
                     sb[r, blk, c : c + 1, :] = rows[blk // 2 : blk // 2 + 1, at : at + 128]
                 sb[r, 4, c : c + 1, :] = rows[2:3, 0:128]
                 sb[r, 5, c : c + 1, :] = rows[3:4, 128:256]
-            start_all(r, *bwd)
 
         def arrived(r, blk, dst, src):
             value = dst[r, blk]
@@ -420,7 +457,7 @@
                 value = jnp.where(sub == blk, src[r, blk], value)
             return value
 
-        def forward(r):
+        def receive(r):
             wait_recv_all(r, *fwd)
             for blk in range(4):
                 value = arrived(r, blk, rf, sf)
@@ -434,36 +471,26 @@
                 pool[c, 23:24, 128:256] = high[c : c + 1]
             fold_pool()
 
-            def group(g, carry):
-                for j in range(8):
-                    fn = g * 8 + j
-                    keep = node_iota2 == nodes[pl.ds(fn, 1), :]
-                    got = dot(pp[...], a_mat[fn])
-                    got = got[:144] + got[144:]
-                    for c in range(6):
-                        nb[c, pl.ds(fn, 1), :] = jnp.sum(
-                            jnp.where(keep, got[24 * c : 24 * c + 24], 0.0), axis=0, keepdims=True
-                        )
-                return carry
-
-            lax.fori_loop(0, FACE // 8, group, 0)
+        def forward(r, whole=True):
             for c in range(6):
                 p[c] = dot(tab[176:216, 0:48], stacked(y[r, c])) - nb[c]
             for at in range(0, FACE, 8):
                 factor = scl[at : at + 8, :]
                 for c, value in enumerate(flux_rows(p, at)):
                     x[c, at : at + 8, :] = value * factor
-            curl_rows([y[r, c] for c in range(3)], [y[r, 3 + c] for c in range(3)])
+            curl_rows(x, [y[r, c] for c in range(3)], [y[r, 3 + c] for c in range(3)])
             for c in range(3):
                 current = (ed * y[r, c] - y[r, 6 + c]) * it
                 k[r, 6 + c] = current
-                k[r, c] = (contracted(0, c) - current) * ie
-                k[r, 3 + c] = contracted(0, 3 + c)
+                k[r, c] = (contracted(x, 0, c) - current) * ie
+                if whole:
+                    k[r, 3 + c] = contracted(x, 0, 3 + c)
 
         def back_volume(r):
             for c in range(6):
-                x[c, 0:40, :] = cd[c]
-            curl_rows([w[r, c] * ie for c in range(3)], [w[r, 3 + c] for c in range(3)])
+                xb[c, 0:40, :] = cd[c]
+            curl_rows(xb, [w[r, c] * ie for c in range(3)], [w[r, 3 + c] for c in range(3)])
+            cots = [contracted(xb, 48, c) for c in range(6)]
             wait_recv_all(r, *bwd)
             for blk in range(BLOCKS):
                 value = arrived(r, blk, rb, sb)
@@ -475,27 +502,15 @@
                 bx[:, 128 * blk : 128 * blk + 128] = jnp.concatenate(high + low, 0).astype(bf16)
             got = dot(bx[...], axt[...])
             s_ref[...] = s_ref[...] + (got[:144] + got[144:])
-            cots = []
             for c in range(6):
-                value = contracted(48, c) + s_ref[24 * c : 24 * c + 24, :]
-                cots.append(jnp.where(own_rows, value, 0.0))
+                value = cots[c] + s_ref[24 * c : 24 * c + 24, :]
+                cots[c] = jnp.where(own_rows, value, 0.0)
             for c in range(3):
                 through = (w[r, 6 + c] - w[r, c] * ie) * it
                 cots[c] = cots[c] + ed * through
                 cots.append(-through)
             return cots
 
-        def one_round(r, ahead, adj_part, back_part):
-            back_faces(r)
-            forward(r)
-            for c in range(9):
-                y[r + 1, c] = y[0, c] + ahead * k[r, c]
-            exports(r + 1)
-            for c, value in enumerate(back_volume(r)):
-                acc[c] = acc[c] + value
-                w[r + 1, c] = adj_part * adj24[c] + back_part * value
-
-        pl.semaphore_wait(barrier, SUBS - 1 + DOMS - 1)
         exports(0)
         index = nbr[...]
         nodes[...] = node_of(index >> 8, faces)
@@ -509,26 +524,52 @@
 
         owners = jnp.transpose(jnp.concatenate([recv[0], jnp.zeros((6, 128), jnp.int32)], axis=0))
         oids[...] = owners
-        lanes = lax.broadcasted_iota(jnp.int32, (DOMS, 128), 1)
-        for q in range(SUBS):
-            ids = oids[pl.ds(q, DOMS, stride=SUBS), :]
+        lanes = lax.broadcasted_iota(jnp.int32, (SITES, 128), 1)
+        for q in range(SEATS):
+            ids = oids[pl.ds((q % 2) * SUBS + q // 2, SITES, stride=SEATS), :]
             for z in range(2):
                 at = 128 * (2 * q + z)
                 oh[:, at : at + 128] = one_hot(lanes == ids[:, z : z + 1])
 
+        def advance(r, ahead):
+            forward(r)
+            for c in range(9):
+                y[r + 1, c] = y[0, c] + ahead * k[r, c]
+            exports(r + 1)
+            start_all(r + 1, *fwd)
+
+        def retreat(r, adj_part, back_part):
+            for c, value in enumerate(back_volume(r)):
+                acc[c] = acc[c] + value
+                w[r + 1, c] = adj_part * adj24[c] + back_part * value
+
+        back_flux(0)
+        sweep(False, True)
+        give_back(0)
+        meet()
+        start_all(0, *fwd)
+        start_all(0, *bwd)
+        receive(0)
+        sweep(True, False)
+        advance(0, 0.5 * time_step)
+        retreat(0, time_step / 3.0, time_step)
+
         def looped(r, carry):
             last = r == 2
-            one_round(
-                r,
-                jnp.where(last, time_step, 0.5 * time_step),
-                jnp.where(last, time_step / 6.0, time_step / 3.0),
-                jnp.where(r == 0, time_step, 0.5 * time_step),
-            )
+            back_flux(r)
+            receive(r)
+            sweep(True, True)
+            give_back(r)
+            start_all(r, *bwd)
+            advance(r, jnp.where(last, time_step, 0.5 * time_step))
+            retreat(r, jnp.where(last, time_step / 6.0, time_step / 3.0), 0.5 * time_step)
             return carry
 
-        lax.fori_loop(0, 3, looped, 0)
-        back_faces(3)
-        forward(3)
+        lax.fori_loop(1, 3, looped, 0)
+        back_flux(3)
+        receive(3)
+        sweep(True, False)
+        forward(3, whole=False)
 
         sums = [jnp.zeros((ROWS, 256), f32) for _ in range(3)]
         for r in range(4):
@@ -542,15 +583,16 @@
             for value, factor in zip(sums, (ie, it, it))
         ]
         slot = sslot[...]
-        target = ((slot >> 1) & 3) * DOMS + (slot >> 3)
+        place = slot >> 1
+        target = ((place & 3) * 2 + ((place >> 2) & 1)) * SITES + (place >> 3)
         chosen = one_hot(lax.broadcasted_iota(jnp.int32, (128, 256), 0) == target)
         lines = [jnp.where((slot & 1) == q, g, 0.0) for q in range(2) for g in grads]
         lines = jnp.concatenate(lines + [jnp.zeros((2, 256), f32)], axis=0)
-        lines = [jnp.where(sub == q, lines, 0.0) for q in range(SUBS)]
-        lines = jnp.concatenate(lines + [jnp.zeros((96, 256), f32)], axis=0)
+        lines = [jnp.where(seat == q, lines, 0.0) for q in range(SEATS)]
+        lines = jnp.concatenate(lines + [jnp.zeros((64, 256), f32)], axis=0)
         packed = sum(dot(chosen, part) for part in parts3(jnp.transpose(lines)))
-        for q in range(SUBS):
-            ya[q] = packed[DOMS * q : DOMS * q + DOMS]
+        for q in range(SEATS):
+            ya[q] = packed[SITES * q : SITES * q + SITES]
 
         def first_hop(to, slot_from):
             return pltpu.make_async_remote_copy(
@@ -558,18 +600,9 @@
                 dst_ref=yr.at[slot_from],
                 send_sem=ps_sem.at[to],
                 recv_sem=pr_sem.at[slot_from],
-                device_id=(dom, to),
+                device_id=seat_device(to),
                 device_id_type=MESH,
             )
-
-        for step in range(1, SUBS):
-            first_hop(lax.rem(sub + step, SUBS), sub).start()
-        for step in range(1, SUBS):
-            other = lax.rem(sub + step, SUBS)
-            first_hop(other, other).wait_recv()
-        mine = ya[pl.ds(sub, 1)][0] + yr[0] + yr[1] + yr[2] + yr[3]
-        for q in range(DOMS):
-            cb[q] = mine[q : q + 1]
 
         def second_hop(to, slot_from):
             return pltpu.make_async_remote_copy(
@@ -577,37 +610,40 @@
                 dst_ref=rc.at[slot_from],
                 send_sem=qs_sem.at[to],
                 recv_sem=qr_sem.at[slot_from],
-                device_id=(to, sub),
+                device_id=site_device(to),
                 device_id_type=MESH,
             )
 
-        def hop_start(step, carry):
-            second_hop(lax.rem(dom + step, DOMS), dom).start()
-            return carry
-
-        def hop_wait(step, carry):
-            other = lax.rem(dom + step, DOMS)
-            second_hop(other, other).wait_recv()
-            return carry
-
-        def hop_sent(step, carry):
-            second_hop(lax.rem(dom + step, DOMS), dom).wait_send()
-            return carry
-
-        lax.fori_loop(1, DOMS, hop_start, 0)
-
+        seats = [lax.rem(seat + step, SEATS) for step in range(1, SEATS)]
+        sites = [lax.rem(site + step, SITES) for step in range(1, SITES)]
+        for other in seats:
+            first_hop(other, seat).start()
+
+        sweep(False, True)
+        give_back(3)
+        start_all(3, *bwd)
+        for other in seats:
+            first_hop(other, other).wait_recv()
+        mine = ya[pl.ds(seat, 1)][0]
+        for q in range(SEATS):
+            mine = mine + yr[q]
+        for q in range(SITES):
+            cb[q] = mine[q : q + 1]
+        for other in sites:
+            second_hop(other, site).start()
         for c, value in enumerate(back_volume(3)):
             out[c] = (acc[c] + value)[:NODES]
 
-        lax.fori_loop(1, DOMS, hop_wait, 0)
-        here = lax.broadcasted_iota(jnp.int32, (DOMS, 128), 0) == dom
-        came = jnp.concatenate([rc[q] for q in range(DOMS)], axis=0)
+        for other in sites:
+            second_hop(other, other).wait_recv()
+        here = lax.broadcasted_iota(jnp.int32, (SITES, 128), 0) == site
+        came = jnp.concatenate([rc[q] for q in range(SITES)], axis=0)
         came = came + jnp.where(here, mine, 0.0)
-        turned = jnp.concatenate(parts3(jnp.transpose(came)[:32]), axis=0)
+        turned = jnp.concatenate(parts3(jnp.transpose(came)[:64]), axis=0)
         spread = dot(turned, oh[...])
-        spread = spread[:32] + spread[32:64] + spread[64:]
+        spread = spread[:64] + spread[64:128] + spread[128:]
         total = jnp.zeros((3, 128), f32)
-        for q in range(SUBS):
+        for q in range(SEATS):
             for z in range(2):
                 row, at = 8 * q + 3 * z, 128 * (2 * q + z)
                 total = total + spread[row : row + 3, at : at + 128]
@@ -616,9 +652,10 @@
         for r in range(4):
             wait_send_all(r, *fwd)
             wait_send_all(r, *bwd)
-        for step in range(1, SUBS):
-            first_hop(lax.rem(sub + step, SUBS), sub).wait_send()
-        lax.fori_loop(1, DOMS, hop_sent, 0)
+        for other in seats:
+            first_hop(other, seat).wait_send()
+        for other in sites:
+            second_hop(other, site).wait_send()
 
     return kernel
 
@@ -666,6 +703,7 @@
         pltpu.VMEM((3, FACE, 256), f32),
         pltpu.VMEM((FACE, 256), f32),
         pltpu.VMEM((6, 112, 256), f32),
+        pltpu.VMEM((6, 112, 256), f32),
         trace, trace, trace,
         pltpu.VMEM((6 * ROWS, 256), f32),
         pltpu.VMEM((6, ROWS, 256), f32),
@@ -676,20 +714,20 @@
         pltpu.VMEM((FACE * 256, 256), bf16),
         pltpu.VMEM((256, 128 * BLOCKS), bf16),
         pltpu.VMEM((128 * BLOCKS, 256), bf16),
-        pltpu.VMEM((12 * ROWS, 2048), bf16),
+        pltpu.VMEM((12 * ROWS, 256 * GROUP), bf16),
         pltpu.VMEM((12 * ROWS, 128 * BLOCKS), bf16),
         pltpu.VMEM((128, 8), jnp.int32),
-        pltpu.VMEM((DOMS, 1024), bf16),
+        pltpu.VMEM((SITES, 128 * 2 * SEATS), bf16),
         message, message, message, message,
-        pltpu.VMEM((SUBS, DOMS, 128), f32),
-        pltpu.VMEM((SUBS, DOMS, 128), f32),
-        pltpu.VMEM((DOMS, 1, 128), f32),
-        pltpu.VMEM((DOMS, 1, 128), f32),
+        pltpu.VMEM((SEATS, SITES, 128), f32),
+        pltpu.VMEM((SEATS, SITES, 128), f32),
+        pltpu.VMEM((SITES, 1, 128), f32),
+        pltpu.VMEM((SITES, 1, 128), f32),
         semaphores, semaphores, semaphores, semaphores,
-        pltpu.SemaphoreType.DMA((SUBS,)),
-        pltpu.SemaphoreType.DMA((SUBS,)),
-        pltpu.SemaphoreType.DMA((DOMS,)),
-        pltpu.SemaphoreType.DMA((DOMS,)),
+        pltpu.SemaphoreType.DMA((SEATS,)),
+        pltpu.SemaphoreType.DMA((SEATS,)),
+        pltpu.SemaphoreType.DMA((SITES,)),
+        pltpu.SemaphoreType.DMA((SITES,)),
     ]
     call = pl.pallas_call(
         kernel_of(faces),

time: 51.2 us -> 55.1 us (1.076)
  Pallas kernels: 49.1 us -> 53 us
    pallas_call x1, Pallas kernels: 49.1 us -> 53 us  [per_device(): call(*[pltpu.with_memory_space_constraint(v, pltpu.HBM) for v in values])]
where the time goes in v3:
time: 55.1 us; the launch traced here: 54.9 us
  Pallas kernels  53 us (96%)
  local copies, waits for them, and re-layouts  1.27 us (2%)
  between operations  0.64 us (1%)
    pallas_call x1, Pallas kernels, per_device(): call(*[pltpu.with_memory_space_constraint(v, pltpu.HBM) for v in values])  53 us
    unnamed x2, local copies, waits for them, and re-layouts  1.27 us

profile of v3, /device:TPU:1, one launch (start us, length us, event | category | flops | bytes accessed | tf_op | source)
XLA Modules:
  0.0 54.9 jit_solution(12146634408385924449)
XLA Ops:
  0.6 53.0 %reverse_step.1 = (f32[9,20,256]{2,1,0:T(8,128)S(1)}, f32[3,64]{1,0:T(4,128)S(1)}) custom-call(f32[9,20,256]{2,1,0:T(8,128)} %refs_0_.1, f32[9,20,256]{2,1,0:T(8,128)} %refs_1_.1, f32[1,256]{1,0:T(1,128)} %bitcast.6, f32[1,256]{1,0:T(1,128)} %bitcast.7, f32[1,256]{1,0:T(1,128)} %bitcast.8, f32[9,256]{1,0:T(8,128)} %refs_5_.1, f32[4,256]{1,0:T(4,128)} %refs_6_.1, ...), custom_call_target="tpu_custom_call" | custom-call | tf_op jit(solution)/shard_map/reverse_step/pallas_call | solution.py:749
  53.7 0.7 %copy.18 = f32[9,20,256]{2,1,0:T(8,128)} copy(f32[9,20,256]{2,1,0:T(8,128)S(1)} %get-tuple-element.4) | data formatting | bytes 368640
  54.4 0.6 %copy.19 = f32[3,64]{1,0:T(4,128)} copy(f32[3,64]{1,0:T(4,128)S(1)} %get-tuple-element.5) | data formatting | bytes 1536

commit v4 on v3

--- a/solution.py
+++ b/solution.py
@@ -198,7 +198,7 @@
         fs, adj, einf, edel, tau, met, fsc, ang, nbr, dexp, sexp, sslot, recv, tab = held
         (
         y, k, w, adj24, acc, nrm, scl, x, xb, p, nb, cd, s_ref, pool, pp, nodes, nodex,
-        a_mat, at_mat, ax, axt, b_mat, bx, oids, oh,
+        elems, a_mat, at_mat, ax, axt, b_mat, bx, oids, oh,
         sf, rf, sb, rb, ya, yr, cb, rc,
         fs_sem, fr_sem, bs_sem, br_sem, ps_sem, pr_sem, qs_sem, qr_sem,
         ) = refs
@@ -511,17 +511,23 @@
                 cots.append(-through)
             return cots
 
-        exports(0)
         index = nbr[...]
         nodes[...] = node_of(index >> 8, faces)
         element = index & 255
-        columns = jnp.transpose(element)
+        elems[...] = element
         lane_iota2 = lax.broadcasted_iota(jnp.int32, (256, 256), 1)
         row_iota2 = lax.broadcasted_iota(jnp.int32, (256, 256), 0)
-        for fn in range(FACE):
-            at_mat[256 * fn : 256 * fn + 256, :] = one_hot(lane_iota2 == columns[:, fn : fn + 1])
-            a_mat[fn] = one_hot(row_iota2 == element[fn : fn + 1])
-
+
+        def build(g, carry):
+            rows = elems[pl.ds(pl.multiple_of(g * 8, 8), 8), :]
+            columns = jnp.transpose(rows)
+            for j in range(8):
+                a_mat[g * 8 + j] = one_hot(row_iota2 == rows[j : j + 1])
+                at = pl.multiple_of(g * 2048 + 256 * j, 256)
+                at_mat[pl.ds(at, 256), :] = one_hot(lane_iota2 == columns[:, j : j + 1])
+            return carry
+
+        lax.fori_loop(0, FACE // 8, build, 0)
         owners = jnp.transpose(jnp.concatenate([recv[0], jnp.zeros((6, 128), jnp.int32)], axis=0))
         oids[...] = owners
         lanes = lax.broadcasted_iota(jnp.int32, (SITES, 128), 1)
@@ -530,69 +536,6 @@
             for z in range(2):
                 at = 128 * (2 * q + z)
                 oh[:, at : at + 128] = one_hot(lanes == ids[:, z : z + 1])
-
-        def advance(r, ahead):
-            forward(r)
-            for c in range(9):
-                y[r + 1, c] = y[0, c] + ahead * k[r, c]
-            exports(r + 1)
-            start_all(r + 1, *fwd)
-
-        def retreat(r, adj_part, back_part):
-            for c, value in enumerate(back_volume(r)):
-                acc[c] = acc[c] + value
-                w[r + 1, c] = adj_part * adj24[c] + back_part * value
-
-        back_flux(0)
-        sweep(False, True)
-        give_back(0)
-        meet()
-        start_all(0, *fwd)
-        start_all(0, *bwd)
-        receive(0)
-        sweep(True, False)
-        advance(0, 0.5 * time_step)
-        retreat(0, time_step / 3.0, time_step)
-
-        def looped(r, carry):
-            last = r == 2
-            back_flux(r)
-            receive(r)
-            sweep(True, True)
-            give_back(r)
-            start_all(r, *bwd)
-            advance(r, jnp.where(last, time_step, 0.5 * time_step))
-            retreat(r, jnp.where(last, time_step / 6.0, time_step / 3.0), 0.5 * time_step)
-            return carry
-
-        lax.fori_loop(1, 3, looped, 0)
-        back_flux(3)
-        receive(3)
-        sweep(True, False)
-        forward(3, whole=False)
-
-        sums = [jnp.zeros((ROWS, 256), f32) for _ in range(3)]
-        for r in range(4):
-            for c in range(3):
-                through = w[3 - r, 6 + c] - w[3 - r, c] * ie
-                sums[0] = sums[0] - w[3 - r, c] * k[r, c]
-                sums[1] = sums[1] + through * y[r, c]
-                sums[2] = sums[2] - through * k[r, 6 + c]
-        grads = [
-            jnp.sum(value, axis=0, keepdims=True) * factor
-            for value, factor in zip(sums, (ie, it, it))
-        ]
-        slot = sslot[...]
-        place = slot >> 1
-        target = ((place & 3) * 2 + ((place >> 2) & 1)) * SITES + (place >> 3)
-        chosen = one_hot(lax.broadcasted_iota(jnp.int32, (128, 256), 0) == target)
-        lines = [jnp.where((slot & 1) == q, g, 0.0) for q in range(2) for g in grads]
-        lines = jnp.concatenate(lines + [jnp.zeros((2, 256), f32)], axis=0)
-        lines = [jnp.where(seat == q, lines, 0.0) for q in range(SEATS)]
-        lines = jnp.concatenate(lines + [jnp.zeros((64, 256), f32)], axis=0)
-        packed = sum(dot(chosen, part) for part in parts3(jnp.transpose(lines)))
-        for q in range(SEATS):
-            ya[q] = packed[SITES * q : SITES * q + SITES]
 
         def first_hop(to, slot_from):
             return pltpu.make_async_remote_copy(
@@ -616,12 +559,68 @@
 
         seats = [lax.rem(seat + step, SEATS) for step in range(1, SEATS)]
         sites = [lax.rem(site + step, SITES) for step in range(1, SITES)]
-        for other in seats:
-            first_hop(other, seat).start()
-
-        sweep(False, True)
-        give_back(3)
-        start_all(3, *bwd)
+        meet()
+
+        def one_round(r, carry):
+            exports(r)
+            start_all(r, *fwd)
+            back_flux(r)
+            sweep(False, True)
+            give_back(r)
+            start_all(r, *bwd)
+            receive(r)
+            sweep(True, False)
+            forward(r)
+
+            @pl.when(r < 3)
+            def _():
+                ahead = jnp.where(r == 2, time_step, 0.5 * time_step)
+                for c in range(9):
+                    y[r + 1, c] = y[0, c] + ahead * k[r, c]
+
+            @pl.when(r == 3)
+            def _():
+                sums = [jnp.zeros((ROWS, 256), f32) for _ in range(3)]
+                for q in range(4):
+                    for c in range(3):
+                        through = w[3 - q, 6 + c] - w[3 - q, c] * ie
+                        sums[0] = sums[0] - w[3 - q, c] * k[q, c]
+                        sums[1] = sums[1] + through * y[q, c]
+                        sums[2] = sums[2] - through * k[q, 6 + c]
+                grads = [
+                    jnp.sum(value, axis=0, keepdims=True) * factor
+                    for value, factor in zip(sums, (ie, it, it))
+                ]
+                slot = sslot[...]
+                place = slot >> 1
+                target = ((place & 3) * 2 + ((place >> 2) & 1)) * SITES + (place >> 3)
+                chosen = one_hot(lax.broadcasted_iota(jnp.int32, (128, 256), 0) == target)
+                lines = [jnp.where((slot & 1) == q, g, 0.0) for q in range(2) for g in grads]
+                lines = jnp.concatenate(lines + [jnp.zeros((2, 256), f32)], axis=0)
+                lines = [jnp.where(seat == q, lines, 0.0) for q in range(SEATS)]
+                lines = jnp.concatenate(lines + [jnp.zeros((64, 256), f32)], axis=0)
+                packed = sum(dot(chosen, part) for part in parts3(jnp.transpose(lines)))
+                for q in range(SEATS):
+                    ya[q] = packed[SITES * q : SITES * q + SITES]
+
+                for other in seats:
+                    first_hop(other, seat).start()
+
+            adj_part = jnp.where(r == 2, time_step / 6.0, time_step / 3.0)
+            back_part = jnp.where(r == 0, time_step, 0.5 * time_step)
+            back = back_volume(r)
+            for c in range(9):
+                acc[c] = acc[c] + back[c]
+
+            @pl.when(r < 3)
+            def _():
+                for c in range(9):
+                    w[r + 1, c] = adj_part * adj24[c] + back_part * back[c]
+
+            return carry
+
+        lax.fori_loop(0, 4, one_round, 0)
+
         for other in seats:
             first_hop(other, other).wait_recv()
         mine = ya[pl.ds(seat, 1)][0]
@@ -631,8 +630,8 @@
             cb[q] = mine[q : q + 1]
         for other in sites:
             second_hop(other, site).start()
-        for c, value in enumerate(back_volume(3)):
-            out[c] = (acc[c] + value)[:NODES]
+        for c in range(9):
+            out[c] = acc[c][:NODES]
 
         for other in sites:
             second_hop(other, other).wait_recv()
@@ -649,9 +648,12 @@
                 total = total + spread[row : row + 3, at : at + 128]
         therm[...] = total[:, :64]
 
-        for r in range(4):
+        def all_sent(r, carry):
             wait_send_all(r, *fwd)
             wait_send_all(r, *bwd)
+            return carry
+
+        lax.fori_loop(0, 4, all_sent, 0)
         for other in seats:
             first_hop(other, seat).wait_send()
         for other in sites:
@@ -710,6 +712,7 @@
         pltpu.VMEM((12 * ROWS, 256), bf16),
         pltpu.VMEM((FACE, 256), jnp.int32),
         pltpu.VMEM((8, 128), jnp.int32),
+        pltpu.VMEM((FACE, 256), jnp.int32),
         pltpu.VMEM((FACE, 256, 256), bf16),
         pltpu.VMEM((FACE * 256, 256), bf16),
         pltpu.VMEM((256, 128 * BLOCKS), bf16),

time: 55.1 us -> 52.4 us (0.951)
  Pallas kernels: 53 us -> 50.3 us
    pallas_call x1, Pallas kernels: 53 us -> 50.3 us  [per_device(): call(*[pltpu.with_memory_space_constraint(v, pltpu.HBM) for v in values])]
where the time goes in v4:
time: 52.4 us; the launch traced here: 52.3 us
  Pallas kernels  50.3 us (96%)
  local copies, waits for them, and re-layouts  1.27 us (2%)
  between operations  0.64 us (1%)
    pallas_call x1, Pallas kernels, per_device(): call(*[pltpu.with_memory_space_constraint(v, pltpu.HBM) for v in values])  50.3 us
    unnamed x2, local copies, waits for them, and re-layouts  1.27 us

profile of v4, /device:TPU:1, one launch (start us, length us, event | category | flops | bytes accessed | tf_op | source)
XLA Modules:
  0.0 52.3 jit_solution(5294895517538135100)
XLA Ops:
  0.6 50.3 %reverse_step.1 = (f32[9,20,256]{2,1,0:T(8,128)S(1)}, f32[3,64]{1,0:T(4,128)S(1)}) custom-call(f32[9,20,256]{2,1,0:T(8,128)} %refs_0_.1, f32[9,20,256]{2,1,0:T(8,128)} %refs_1_.1, f32[1,256]{1,0:T(1,128)} %bitcast.6, f32[1,256]{1,0:T(1,128)} %bitcast.7, f32[1,256]{1,0:T(1,128)} %bitcast.8, f32[9,256]{1,0:T(8,128)} %refs_5_.1, f32[4,256]{1,0:T(4,128)} %refs_6_.1, ...), custom_call_target="tpu_custom_call" | custom-call | tf_op jit(solution)/shard_map/reverse_step/pallas_call | solution.py:752
  51.0 0.7 %copy.18 = f32[9,20,256]{2,1,0:T(8,128)} copy(f32[9,20,256]{2,1,0:T(8,128)S(1)} %get-tuple-element.4) | data formatting | bytes 368640
  51.7 0.6 %copy.19 = f32[3,64]{1,0:T(4,128)} copy(f32[3,64]{1,0:T(4,128)S(1)} %get-tuple-element.5) | data formatting | bytes 1536

commit v5 on v4

--- a/solution.py
+++ b/solution.py
@@ -559,11 +559,11 @@
 
         seats = [lax.rem(seat + step, SEATS) for step in range(1, SEATS)]
         sites = [lax.rem(site + step, SITES) for step in range(1, SITES)]
+        exports(0)
         meet()
+        start_all(0, *fwd)
 
         def one_round(r, carry):
-            exports(r)
-            start_all(r, *fwd)
             back_flux(r)
             sweep(False, True)
             give_back(r)
@@ -577,6 +577,8 @@
                 ahead = jnp.where(r == 2, time_step, 0.5 * time_step)
                 for c in range(9):
                     y[r + 1, c] = y[0, c] + ahead * k[r, c]
+                exports(r + 1)
+                start_all(r + 1, *fwd)
 
             @pl.when(r == 3)
             def _():

time: 52.4 us -> 50.1 us (0.956)
  Pallas kernels: 50.3 us -> 48.1 us
    pallas_call x1, Pallas kernels: 50.3 us -> 48.1 us  [per_device(): call(*[pltpu.with_memory_space_constraint(v, pltpu.HBM) for v in values])]
where the time goes in v5:
time: 50.1 us; the launch traced here: 50 us
  Pallas kernels  48.1 us (96%)
  local copies, waits for them, and re-layouts  1.27 us (3%)
  between operations  0.64 us (1%)
    pallas_call x1, Pallas kernels, per_device(): call(*[pltpu.with_memory_space_constraint(v, pltpu.HBM) for v in values])  48.1 us
    unnamed x2, local copies, waits for them, and re-layouts  1.27 us

profile of v5, /device:TPU:1, one launch (start us, length us, event | category | flops | bytes accessed | tf_op | source)
XLA Modules:
  0.0 50.0 jit_solution(8738555410540378799)
XLA Ops:
  0.6 48.1 %reverse_step.1 = (f32[9,20,256]{2,1,0:T(8,128)S(1)}, f32[3,64]{1,0:T(4,128)S(1)}) custom-call(f32[9,20,256]{2,1,0:T(8,128)} %refs_0_.1, f32[9,20,256]{2,1,0:T(8,128)} %refs_1_.1, f32[1,256]{1,0:T(1,128)} %bitcast.6, f32[1,256]{1,0:T(1,128)} %bitcast.7, f32[1,256]{1,0:T(1,128)} %bitcast.8, f32[9,256]{1,0:T(8,128)} %refs_5_.1, f32[4,256]{1,0:T(4,128)} %refs_6_.1, ...), custom_call_target="tpu_custom_call" | custom-call | tf_op jit(solution)/shard_map/reverse_step/pallas_call | solution.py:754
  48.7 0.7 %copy.18 = f32[9,20,256]{2,1,0:T(8,128)} copy(f32[9,20,256]{2,1,0:T(8,128)S(1)} %get-tuple-element.4) | data formatting | bytes 368640
  49.4 0.6 %copy.19 = f32[3,64]{1,0:T(4,128)} copy(f32[3,64]{1,0:T(4,128)S(1)} %get-tuple-element.5) | data formatting | bytes 1536

commit v6 on v5

--- a/solution.py
+++ b/solution.py
@@ -19,7 +19,7 @@
 BLOCKS = 6
 SEATS = 8
 SITES = 16
-GROUP = 8
+GROUP = 20
 MESH = pl.DeviceIdType.MESH
 
 

time: 50.1 us -> 47.8 us (0.954)
  Pallas kernels: 48.1 us -> 45.8 us
    pallas_call x1, Pallas kernels: 48.1 us -> 45.8 us  [per_device(): call(*[pltpu.with_memory_space_constraint(v, pltpu.HBM) for v in values])]
where the time goes in v6:
time: 47.8 us; the launch traced here: 47.7 us
  Pallas kernels  45.8 us (96%)
  local copies, waits for them, and re-layouts  1.27 us (3%)
  between operations  0.64 us (1%)
    pallas_call x1, Pallas kernels, per_device(): call(*[pltpu.with_memory_space_constraint(v, pltpu.HBM) for v in values])  45.8 us
    unnamed x2, local copies, waits for them, and re-layouts  1.27 us

profile of v6, /device:TPU:1, one launch (start us, length us, event | category | flops | bytes accessed | tf_op | source)
XLA Modules:
  0.0 47.7 jit_solution(10807979591792673991)
XLA Ops:
  0.6 45.8 %reverse_step.1 = (f32[9,20,256]{2,1,0:T(8,128)S(1)}, f32[3,64]{1,0:T(4,128)S(1)}) custom-call(f32[9,20,256]{2,1,0:T(8,128)} %refs_0_.1, f32[9,20,256]{2,1,0:T(8,128)} %refs_1_.1, f32[1,256]{1,0:T(1,128)} %bitcast.6, f32[1,256]{1,0:T(1,128)} %bitcast.7, f32[1,256]{1,0:T(1,128)} %bitcast.8, f32[9,256]{1,0:T(8,128)} %refs_5_.1, f32[4,256]{1,0:T(4,128)} %refs_6_.1, ...), custom_call_target="tpu_custom_call" | custom-call | tf_op jit(solution)/shard_map/reverse_step/pallas_call | solution.py:754
  46.4 0.7 %copy.18 = f32[9,20,256]{2,1,0:T(8,128)} copy(f32[9,20,256]{2,1,0:T(8,128)S(1)} %get-tuple-element.4) | data formatting | bytes 368640
  47.1 0.6 %copy.19 = f32[3,64]{1,0:T(4,128)} copy(f32[3,64]{1,0:T(4,128)S(1)} %get-tuple-element.5) | data formatting | bytes 1536

commit v7 on v6

--- a/solution.py
+++ b/solution.py
@@ -19,7 +19,7 @@
 BLOCKS = 6
 SEATS = 8
 SITES = 16
-GROUP = 20
+GROUP = 40
 MESH = pl.DeviceIdType.MESH
 
 

time: 47.8 us -> 54.9 us (1.15)
  Pallas kernels: 45.8 us -> 52.8 us
    pallas_call x1, Pallas kernels: 45.8 us -> 52.8 us  [per_device(): call(*[pltpu.with_memory_space_constraint(v, pltpu.HBM) for v in values])]
where the time goes in v7:
time: 54.9 us; the launch traced here: 54.7 us
  Pallas kernels  52.8 us (96%)
  local copies, waits for them, and re-layouts  1.27 us (2%)
  between operations  0.64 us (1%)
    pallas_call x1, Pallas kernels, per_device(): call(*[pltpu.with_memory_space_constraint(v, pltpu.HBM) for v in values])  52.8 us
    unnamed x2, local copies, waits for them, and re-layouts  1.27 us

profile of v7, /device:TPU:1, one launch (start us, length us, event | category | flops | bytes accessed | tf_op | source)
XLA Modules:
  0.0 54.7 jit_solution(4524558273218940393)
XLA Ops:
  0.6 52.8 %reverse_step.1 = (f32[9,20,256]{2,1,0:T(8,128)S(1)}, f32[3,64]{1,0:T(4,128)S(1)}) custom-call(f32[9,20,256]{2,1,0:T(8,128)} %refs_0_.1, f32[9,20,256]{2,1,0:T(8,128)} %refs_1_.1, f32[1,256]{1,0:T(1,128)} %bitcast.6, f32[1,256]{1,0:T(1,128)} %bitcast.7, f32[1,256]{1,0:T(1,128)} %bitcast.8, f32[9,256]{1,0:T(8,128)} %refs_5_.1, f32[4,256]{1,0:T(4,128)} %refs_6_.1, ...), custom_call_target="tpu_custom_call" | custom-call | tf_op jit(solution)/shard_map/reverse_step/pallas_call | solution.py:754
  53.5 0.7 %copy.18 = f32[9,20,256]{2,1,0:T(8,128)} copy(f32[9,20,256]{2,1,0:T(8,128)S(1)} %get-tuple-element.4) | data formatting | bytes 368640
  54.1 0.6 %copy.19 = f32[3,64]{1,0:T(4,128)} copy(f32[3,64]{1,0:T(4,128)S(1)} %get-tuple-element.5) | data formatting | bytes 1536

commit v8 on v6

--- a/solution.py
+++ b/solution.py
@@ -409,9 +409,11 @@
                     cd[c, at : at + 8, :] = value
 
         def sweep(gather, scatter):
+            rows_a_step = GROUP if scatter else FACE
+
             def group(g, carry):
-                for j in range(GROUP):
-                    fn = g * GROUP + j
+                for j in range(rows_a_step):
+                    fn = g * rows_a_step + j
                     keep = node_iota2 == nodes[pl.ds(fn, 1), :]
                     if gather:
                         got = dot(pp[...], a_mat[fn])
@@ -440,7 +442,7 @@
 
             if scatter:
                 s_ref[...] = jnp.zeros_like(s_ref)
-            lax.fori_loop(0, FACE // GROUP, group, 0)
+            lax.fori_loop(0, FACE // rows_a_step, group, 0)
 
         def give_back(r):
             for c in range(6):

time: 47.8 us -> 46.6 us (0.975)
  Pallas kernels: 45.8 us -> 44.5 us
    pallas_call x1, Pallas kernels: 45.8 us -> 44.5 us  [per_device(): call(*[pltpu.with_memory_space_constraint(v, pltpu.HBM) for v in values])]
where the time goes in v8:
time: 46.6 us; the launch traced here: 46.5 us
  Pallas kernels  44.5 us (95%)
  local copies, waits for them, and re-layouts  1.27 us (3%)
  between operations  0.64 us (1%)
    pallas_call x1, Pallas kernels, per_device(): call(*[pltpu.with_memory_space_constraint(v, pltpu.HBM) for v in values])  44.5 us
    unnamed x2, local copies, waits for them, and re-layouts  1.27 us

profile of v8, /device:TPU:1, one launch (start us, length us, event | category | flops | bytes accessed | tf_op | source)
XLA Modules:
  0.0 46.5 jit_solution(5909196066087664202)
XLA Ops:
  0.6 44.5 %reverse_step.1 = (f32[9,20,256]{2,1,0:T(8,128)S(1)}, f32[3,64]{1,0:T(4,128)S(1)}) custom-call(f32[9,20,256]{2,1,0:T(8,128)} %refs_0_.1, f32[9,20,256]{2,1,0:T(8,128)} %refs_1_.1, f32[1,256]{1,0:T(1,128)} %bitcast.6, f32[1,256]{1,0:T(1,128)} %bitcast.7, f32[1,256]{1,0:T(1,128)} %bitcast.8, f32[9,256]{1,0:T(8,128)} %refs_5_.1, f32[4,256]{1,0:T(4,128)} %refs_6_.1, ...), custom_call_target="tpu_custom_call" | custom-call | tf_op jit(solution)/shard_map/reverse_step/pallas_call | solution.py:756
  45.2 0.7 %copy.18 = f32[9,20,256]{2,1,0:T(8,128)} copy(f32[9,20,256]{2,1,0:T(8,128)S(1)} %get-tuple-element.4) | data formatting | bytes 368640
  45.9 0.6 %copy.19 = f32[3,64]{1,0:T(4,128)} copy(f32[3,64]{1,0:T(4,128)S(1)} %get-tuple-element.5) | data formatting | bytes 1536
